TPU v7x, 128 devices: a whole 4x4x4 slice. The times are simulated.
128 devices in a mesh: row: 8 (over z, x_lo), col: 16 (over x_hi, y, core).
Axes of the slice: x: 4 (x_hi: 2, x_lo: 2; x = x_hi * 2 + x_lo), y: 4, z: 4, core: 2. Of those that a mesh axis runs over, the one named last changes fastest.
Arguments:
- front: float32 [62464, 2048], P('row', 'col')
- child_update: bfloat16 [62464, 2048], P('row', 'col'), may hold values from -6 to 6
- child_rows: int32 [4, 244], replicated, may hold values from 16 to 487, as said below
Outputs:
- factor: float32 [62464, 2048], P('row', 'col')
Inputs may be any that keep to these rules, and one draw needn't show every extreme that they name: `child_rows`: each row names 244 distinct parent block rows, none below 16. Block row b of child c lies on row group (c // 2) * 4 + b // 61; the 61 block rows of one row group go to the parent row groups (each owning 61 consecutive block rows) in turn, from a drawn first one, so at most 8 of them reach one parent row group.
All inputs are finite; a program needn't handle non-finite values.
Results may differ from a plain program's by a relative error of at most 0.0017.
Values may be sent and summed in bfloat16 or wider, within the bound.
No kernel may reach another device: no remote copies, remote signals or barrier semaphores. Data moves between devices by JAX's collectives and lax.ppermute only.
A program may use at most 128 MiB of HBM per device.

v0:
```python
import jax
import jax.numpy as jnp
from jax import lax
from jax.sharding import PartitionSpec as P

CR = 31232
STEPS = 3


def from_root(block, axis, owner):
    block = jnp.where(lax.axis_index(axis) == owner, block, jnp.zeros_like(block))
    return lax.psum(block, axis)


def on_device(front, child_update, child_rows):
    block_cols = front.shape[1]
    local_rows = front.shape[0]
    row_blocks = local_rows // block_cols
    col_count = lax.axis_size("col")
    row_here = lax.axis_index("row")
    col_here = lax.axis_index("col")
    col_half = col_here // (col_count // 2)
    child_total_blocks = CR // block_cols

    def rows_single(running, shard_rows, first_row):
        row_total = shard_rows.shape[0]
        child_row = jnp.arange(row_total, dtype=jnp.int32)
        owner_half = child_row // CR
        child_block = child_row % CR // block_cols
        target = child_rows[2 * owner_half + col_half, child_block]
        usable = target // row_blocks == row_here
        destination = jnp.where(
            usable, target % row_blocks * block_cols + child_row % block_cols, local_rows
        )
        return running.at[destination].add(shard_rows.astype(jnp.float32), mode="drop")

    def rows_blocked(running, shard_rows, first_row):
        tile_count = shard_rows.shape[0] // block_cols
        block_index = jnp.arange(tile_count, dtype=jnp.int32)
        owner_half = block_index // child_total_blocks
        child_block = block_index % child_total_blocks
        target = child_rows[2 * owner_half + col_half, child_block]
        usable = target // row_blocks == row_here
        destination = jnp.where(usable, target % row_blocks, row_blocks)
        tiles = shard_rows.reshape(tile_count, block_cols, block_cols)
        tiles = jnp.where(usable[:, None, None], tiles, jnp.zeros((), jnp.bfloat16)).astype(
            jnp.float32
        )
        grid = (
            running.reshape(row_blocks, block_cols, block_cols)
            .at[destination]
            .add(tiles, mode="drop")
        )
        return grid.reshape(local_rows, block_cols)

    first_row = jnp.int32(0)
    contribution = lax.cond(
        first_row % block_cols == 0,
        rows_blocked,
        rows_single,
        jnp.zeros((local_rows, block_cols), jnp.float32),
        lax.all_gather(child_update, "row", axis=0, tiled=True),
        first_row,
    )
    working = front + contribution
    global_rows = row_here * local_rows + jnp.arange(local_rows, dtype=jnp.int32)[:, None]
    identity = jnp.eye(block_cols, dtype=jnp.float32)
    factor = jnp.zeros((local_rows, block_cols), jnp.float32)
    for panel_step in range(STEPS):
        first_col = panel_step * block_cols
        corner = from_root(working[first_col : first_col + block_cols], "row", 0)
        corner = jnp.where(col_here == panel_step, corner, identity)
        symmetric = jnp.tril(corner) + jnp.tril(corner, -1).T
        lower_factor = jnp.linalg.cholesky(symmetric)
        solved = jax.scipy.linalg.solve_triangular(lower_factor, working.T, lower=True).T
        placed = (
            jnp.zeros((local_rows, block_cols), jnp.float32)
            .at[first_col : first_col + block_cols]
            .set(lower_factor)
        )
        panel_cols = jnp.where(
            global_rows < first_col,
            0.0,
            jnp.where(global_rows < first_col + block_cols, placed, solved),
        )
        factor = jnp.where(col_here == panel_step, panel_cols, factor)
        narrow = from_root(panel_cols.astype(jnp.bfloat16), "col", panel_step)
        slab_part = lax.dynamic_slice_in_dim(narrow, col_here * block_cols, block_cols, 0)
        slab_part = from_root(slab_part, "row", 0)
        update = jnp.dot(narrow, slab_part.T, preferred_element_type=jnp.float32)
        working = jnp.where(col_here > panel_step, working - update, working)
    result = jnp.where(col_here < STEPS, factor, working)
    global_cols = col_here * block_cols + jnp.arange(block_cols, dtype=jnp.int32)[None, :]
    return jnp.where(global_rows >= global_cols, result, 0.0)


def solution(mesh):
    in_specs = (P("row", "col"), P("row", "col"), P())
    out_specs = P("row", "col")
    return jax.shard_map(
        on_device, mesh=mesh, in_specs=in_specs, out_specs=out_specs, check_vma=False
    )
```

profile of v0, /device:TPU:0, one launch (start us, length us, event | category | flops | bytes accessed | tf_op | source)
XLA Modules:
  0.0 1335.6 jit_solution(5442505958227239122)
XLA Ops:
  6.5 0.7 all-gather.2.cloned.1.call-update
  7.4 6.8 gather_fusion
  14.2 308.1 %all-gather.2.cloned.1.call-done = bf16[62464,128]{1,0:T(8,128)(2,1)} async-done(((bf16[7808,128]{1,0:T(8,128)(2,1)}), bf16[62464,128]{1,0:T(8,128)(2,1)}) %all-gather.2.cloned.1.call-update) | async-done | bytes 15990800 | tf_op jit(solution)/shard_map/all_gather | solution.py:62
  322.3 18.0 %select_convert_fusion = f32[488,128,128]{2,1,0:T(8,128)} fusion(bf16[488,128,128]{2,1,0:T(8,128)(2,1)} %bitcast.86, pred[488]{0:T(512)(128)(4,1)S(1)} %get-tuple-element.62), kind=kLoop, calls=%fused_computation.2 | loop fusion | flops 15990784 | bytes 47972840 | tf_op jit(solution)/shard_map/cond/branch_1_fun/convert_element_type | solution.py:46
  340.3 2.4 cond.9
  342.8 106.0 %scatter_fusion = f32[61,128,128]{2,1,0:T(8,128)} fusion(f32[61,128,128]{2,1,0:T(8,128)} %cond.9, s32[488]{0:T(512)S(1)} %bitcast.87, f32[488,128,128]{2,1,0:T(8,128)} %select_convert_fusion), kind=kCustom, calls=%fused_computation.1 | custom fusion | flops 7995392 | bytes 95946656 | tf_op jit(solution)/shard_map/cond/branch_1_fun/scatter-add | solution.py:52
  448.7 3.8 bitcast_add_fusion
  452.5 1.9 copy-done.3
  454.4 0.6 slice_select_fusion.2
  455.1 74.9 %all-reduce.10.cloned.1.call-done = f32[128,128]{1,0:T(8,128)} async-done(((f32[128,128]{1,0:T(8,128)}), f32[128,128]{1,0:T(8,128)}) %all-reduce.10.cloned.1.call-update) | async-done | bytes 65552 | tf_op jit(solution)/shard_map/psum | solution.py:12
  530.0 0.9 convert_select_fusion.5
  531.0 0.9 bitcast_add_fusion.6
  532.0 11.7 cholesky.59
  543.8 0.7 compare_reduce_fusion.2
  544.5 0.7 fusion.28
  545.2 9.8 custom-call.9
  555.0 11.4 convert_select_fusion.2
  566.6 0.1 copy.30
  566.8 0.1 copy.28
  566.9 141.0 %all-reduce.12.cloned.1.call-done = bf16[7808,128]{1,0:T(8,128)(2,1)} async-done(((bf16[7808,128]{1,0:T(8,128)(2,1)}), bf16[7808,128]{1,0:T(8,128)(2,1)}) %all-reduce.12.cloned.1.call-update) | async-done | bytes 1998864 | tf_op jit(solution)/shard_map/psum | solution.py:12
  707.9 0.8 dynamic-slice_select_fusion.2
  708.7 34.6 %psum.65 = bf16[128,128]{1,0:T(8,128)(2,1)S(1)} all-reduce(bf16[128,128]{1,0:T(8,128)(2,1)S(1)} %dynamic-slice_select_fusion.2), channel_id=1, replica_groups=mesh['row'=8,'col'=16] {'row'}, use_global_device_ids=true, to_apply=%region_5.8 | all-reduce | flops 16384 | bytes 65536 | tf_op jit(solution)/shard_map/psum | solution.py:12
  743.3 3.4 fusion.2
  746.7 1.9 copy-done.4
  748.7 0.6 slice_select_fusion.1
  749.4 69.9 %all-reduce.14.cloned.1.call-done = f32[128,128]{1,0:T(8,128)} async-done(((f32[128,128]{1,0:T(8,128)}), f32[128,128]{1,0:T(8,128)}) %all-reduce.14.cloned.1.call-update) | async-done | bytes 65552 | tf_op jit(solution)/shard_map/psum | solution.py:12
  819.7 11.7 cholesky.70
  831.4 0.6 compare_reduce_fusion.1
  832.1 0.6 fusion.29
  832.7 9.8 custom-call.10
  842.5 11.6 convert_select_fusion.1
  854.2 142.9 %all-reduce.16.cloned.1.call-done = bf16[7808,128]{1,0:T(8,128)(2,1)} async-done(((bf16[7808,128]{1,0:T(8,128)(2,1)}), bf16[7808,128]{1,0:T(8,128)(2,1)}) %all-reduce.16.cloned.1.call-update) | async-done | bytes 1998864 | tf_op jit(solution)/shard_map/psum | solution.py:12
  997.1 0.8 dynamic-slice_select_fusion.1
  997.9 34.6 %psum.68 = bf16[128,128]{1,0:T(8,128)(2,1)S(1)} all-reduce(bf16[128,128]{1,0:T(8,128)(2,1)S(1)} %dynamic-slice_select_fusion.1), channel_id=1, replica_groups=mesh['row'=8,'col'=16] {'row'}, use_global_device_ids=true, to_apply=%region_8.11 | all-reduce | flops 16384 | bytes 65536 | tf_op jit(solution)/shard_map/psum | solution.py:12
  1032.5 3.4 fusion.1
  1035.9 1.9 copy-done.2
  1037.8 0.6 slice_select_fusion
  1038.5 0.3 all-reduce.20.cloned.1.call-start
  1038.8 69.7 %all-reduce.18.cloned.1.call-done = f32[128,128]{1,0:T(8,128)} async-done(((f32[128,128]{1,0:T(8,128)}), f32[128,128]{1,0:T(8,128)}) %all-reduce.18.cloned.1.call-update) | async-done | bytes 65552 | tf_op jit(solution)/shard_map/psum | solution.py:12
  1108.8 11.7 cholesky.81
  1120.6 0.6 compare_reduce_fusion
  1121.2 0.6 select_bitcast_fusion
  1121.7 9.8 custom-call.11
  1131.5 11.8 convert_select_fusion
  1143.4 142.9 %all-reduce.20.cloned.1.call-done = bf16[7808,128]{1,0:T(8,128)(2,1)} async-done(((bf16[7808,128]{1,0:T(8,128)(2,1)}), bf16[7808,128]{1,0:T(8,128)(2,1)}) %all-reduce.20.cloned.1.call-update) | async-done | bytes 1998864 | tf_op jit(solution)/shard_map/psum | solution.py:12
  1286.3 0.8 dynamic-slice_select_fusion
  1287.1 34.6 %psum.71 = bf16[128,128]{1,0:T(8,128)(2,1)S(1)} all-reduce(bf16[128,128]{1,0:T(8,128)(2,1)S(1)} %dynamic-slice_select_fusion), channel_id=1, replica_groups=mesh['row'=8,'col'=16] {'row'}, use_global_device_ids=true, to_apply=%region_11.14 | all-reduce | flops 16384 | bytes 65536 | tf_op jit(solution)/shard_map/psum | solution.py:12
  1321.7 7.0 fusion.10
  (48 shorter events, 1.5 us)
Async XLA Ops:
  6.5 0.8 copy-start
  6.5 315.8 %all-gather.2.cloned.1.call-start = ((), (), s32[]{:S(2)}) async-start(), calls=%async_computation | async-start | bytes 17989632 | tf_op jit(solution)/shard_map/all_gather | solution.py:62
  7.3 522.8 %all-reduce.10.cloned.1.call-start = ((), (), s32[]{:S(2)}) async-start(), calls=%async_computation.1 | async-start | bytes 131072 | tf_op jit(solution)/shard_map/psum | solution.py:12
  452.5 1.9 copy-start.3
  455.1 252.8 %all-reduce.12.cloned.1.call-start = ((), (), s32[]{:S(2)}) async-start(), calls=%async_computation.2 | async-start | bytes 3997696 | tf_op jit(solution)/shard_map/psum | solution.py:12
  566.5 252.8 %all-reduce.14.cloned.1.call-start = ((), (), s32[]{:S(2)}) async-start(), calls=%async_computation.3 | async-start | bytes 131072 | tf_op jit(solution)/shard_map/psum | solution.py:12
  746.7 1.9 copy-start.4
  749.3 247.8 %all-reduce.16.cloned.1.call-start = ((), (), s32[]{:S(2)}) async-start(), calls=%async_computation.4 | async-start | bytes 3997696 | tf_op jit(solution)/shard_map/psum | solution.py:12
  854.1 254.4 %all-reduce.18.cloned.1.call-start = ((), (), s32[]{:S(2)}) async-start(), calls=%async_computation.5 | async-start | bytes 131072 | tf_op jit(solution)/shard_map/psum | solution.py:12
  1035.9 1.9 copy-start.2
  1038.5 247.9 %all-reduce.20.cloned.1.call-start = ((), (), s32[]{:S(2)}) async-start(), calls=%async_computation.6 | async-start | bytes 3997696 | tf_op jit(solution)/shard_map/psum | solution.py:12
  1321.7 7.0 copy-start.1
Sparse Core Ops, SparseCore 0:
  9.0 313.3 all-gather.1
  455.2 74.7 all-reduce.9
  566.6 141.2 all-reduce.11
  749.5 69.8 all-reduce.13
  854.2 142.8 all-reduce.15
  1038.6 69.8 all-reduce.17
  1143.5 142.8 all-reduce.19
where the time goes:
time: 1340 us
  waiting for transfers between devices  950 us (71%)
  other arithmetic  203 us (15%)
  blocking collectives  104 us (8%)
  matrix products  48.7 us (4%)
  local copies, waits for them, and re-layouts  15.9 us (1%)
  between operations  13.8 us (1%)
    psum x6, waiting for transfers between devices, from_root(): return lax.psum(block, axis)  641 us
    all_gather x1, waiting for transfers between devices, on_device(): lax.all_gather(child_update, 'row', axis=0, tiled=True)  308 us
    scatter-add x1, other arithmetic, rows_blocked(): grid = running.reshape(row_blocks, block_cols, block_cols).at[destination...  106 us
    psum x3, blocking collectives, from_root(): return lax.psum(block, axis)  104 us
    another operation x9, other arithmetic, on_device(): lower_factor = jnp.linalg.cholesky(symmetric)  37.2 us
    another operation x3, matrix products, on_device(): jax.scipy.linalg.solve_triangular(lower_factor, working.T, lower=True)  34.8 us
    another operation x6, other arithmetic, on_device(): jax.scipy.linalg.solve_triangular(lower_factor, working.T, lower=True)  31.3 us
  transfers between devices with their start and end apart: 7, of which 7 were waited for; matrix products, arithmetic and copies ran while one was open for 1% of the time, Pallas kernels for 0%

commit v1 on v0

v1 whole, which is shorter than its diff:
```python
import functools

import jax
import jax.numpy as jnp
from jax import lax
from jax.experimental import pallas as pl
from jax.experimental.pallas import tpu as pltpu
from jax.sharding import PartitionSpec as P


B = 128
STEPS = 3
RB = 61
ROWS = RB * B
NR = 8
NC = 16
TOP = NC
CH = 4
NQ = NC // 2
F32 = jnp.float32
BF16 = jnp.bfloat16
HI = lax.Precision.HIGHEST
VM = pl.BlockSpec(memory_space=pltpu.VMEM)
SM = pl.BlockSpec(memory_space=pltpu.SMEM)
ANY = pl.BlockSpec(memory_space=pl.ANY)


def params(mib=56):
    return pltpu.CompilerParams(vmem_limit_bytes=mib * 1024 * 1024)


def cost(us):
    return pl.CostEstimate(flops=int(us * 9e8), bytes_accessed=int(us * 3e6), transcendentals=0)


def dot_t(a, b, precision=None):
    return lax.dot_general(
        a, b, (((1,), (1,)), ((), ())), precision=precision, preferred_element_type=F32
    )


def chunk_block(owner, t):
    return owner if t == 0 else TOP + 3 * owner + t - 1


def pack_kernel(pos, rows, child, out, sems):
    row, half = pos[0], pos[1] // (NC // 2)
    c, g = 2 * (row // (NR // 2)) + half, row % (NR // 2)
    first = rows[c, g * RB] // RB
    copies = []
    for d in range(NR):
        residue = (d - first + NR) % NR
        for s in range(NR):
            p = jnp.minimum(NR * s + residue, RB - 1)
            copies.append(
                pltpu.make_async_copy(
                    child.at[pl.ds(pl.multiple_of(p * B, B), B)],
                    out.at[pl.ds((d * NR + s) * B, B)],
                    sems.at[d * NR + s],
                )
            )
            copies[-1].start()
    for copy in copies:
        copy.wait()


def pack(pos, rows, child):
    return pl.pallas_call(
        pack_kernel,
        out_shape=jax.ShapeDtypeStruct((NR * NR * B, B), BF16),
        in_specs=[SM, SM, ANY],
        out_specs=VM,
        scratch_shapes=[pltpu.SemaphoreType.DMA((NR * NR,))],
        compiler_params=params(),
        cost_estimate=cost(3),
        name="pack",
    )(pos, rows, child)


def assemble_kernel(pos, rows, front, got, work, *chunks):
    row, col = pos[0], pos[1]
    half = col // (NC // 2)
    work[...] = front[...]
    for src in range(NR):
        c, g = 2 * (src // (NR // 2)) + half, src % (NR // 2)
        first = rows[c, g * RB] // RB
        residue = (row - first + NR) % NR

        def add(s, carry, src=src, c=c, g=g, residue=residue):
            p = NR * s + residue

            @pl.when(p < RB)
            def _():
                b = rows[c, g * RB + jnp.minimum(p, RB - 1)] - row * RB
                at = pl.ds(pl.multiple_of(b * B, B), B)
                piece = got[pl.ds(pl.multiple_of((src * NR + s) * B, B), B)]
                work[at] = work[at] + piece.astype(F32)

            return carry

        lax.fori_loop(0, NR, add, 0)

    @pl.when(col < STEPS)
    def _():
        for s in range(NQ):
            chip = (col // 8 + s // 4) % 2 * 4 + (col // 2 + s) % 4
            for c in range(2):
                for t in range(CH):
                    b = jnp.minimum(chunk_block(2 * chip + c, t), RB - 1)
                    at = (c * CH + t) * B
                    chunks[s][at : at + B] = work[pl.ds(pl.multiple_of(b * B, B), B)]


def assemble(pos, rows, front, got):
    return pl.pallas_call(
        assemble_kernel,
        out_shape=[jax.ShapeDtypeStruct((ROWS, B), F32)]
        + [jax.ShapeDtypeStruct((2 * CH * B, B), F32)] * NQ,
        in_specs=[SM, SM, VM, VM],
        out_specs=[VM] * (NQ + 1),
        compiler_params=params(),
        cost_estimate=cost(6),
        name="assemble",
    )(pos, rows, front, got)


NB = 32
NW = 8


def eliminate(m):
    sub = lax.broadcasted_iota(jnp.int32, (NB, B), 0)
    for lo in range(0, B, NB):
        halves = [m[lo : lo + NB, :B], m[lo : lo + NB, B:]]
        for t in range(0, NB, NW):
            spread = [
                jnp.broadcast_to(halves[0][:, lo + t + i : lo + t + i + 1], (NB, B))
                for i in range(NW)
            ]
            lines = [[h[t + i : t + i + 1] for h in halves] for i in range(NW)]
            for i in range(NW):
                scale = lax.rsqrt(spread[i][t + i : t + i + 1])
                spread[i] = spread[i] * scale
                lines[i] = [line * scale for line in lines[i]]
                for n in range(i + 1, NW):
                    ratio = spread[i][t + n : t + n + 1]
                    spread[n] = spread[n] - spread[i] * ratio
                    lines[n] = [a - ratio * b for a, b in zip(lines[n], lines[i], strict=True)]
            for i in range(NW):
                ratio = jnp.where(sub >= t + NW, spread[i], 0.0)
                halves = [h - ratio * line for h, line in zip(halves, lines[i], strict=True)]
            for i in range(NW):
                halves = [
                    jnp.where(sub == t + i, line, h)
                    for h, line in zip(halves, lines[i], strict=True)
                ]
        r = jnp.concatenate(halves, axis=1)
        m[lo : lo + NB] = r
        if lo + NB < B:
            m[lo + NB :] = m[lo + NB :] - lax.dot_general(
                r[:, lo + NB : B],
                r,
                (((0,), (0,)), ((), ())),
                precision=HI,
                preferred_element_type=F32,
            )


def factor_kernel(top, low, inv, facing, m):
    lane = lax.broadcasted_iota(jnp.int32, (B, B), 1)
    sub = lax.broadcasted_iota(jnp.int32, (B, B), 0)

    def load(a):
        m[:, :B] = jnp.where(sub >= lane, a, a.T)
        m[:, B:] = jnp.where(lane == sub, 1.0, 0.0).astype(F32)

    def part(i):
        return top[i * B : (i + 1) * B]

    load(part(0))

    def step(k, carry):
        eliminate(m)
        low[k] = jnp.where(lane >= sub, m[:, :B], 0.0).T
        inverse = m[:, B:]
        inv[k] = inverse

        @pl.when(k == 0)
        def _():
            n01 = dot_t(part(1), inverse, HI).astype(BF16)
            facing[0] = n01
            facing[1] = dot_t(part(2), inverse, HI).astype(BF16)
            load(part(3) - dot_t(n01, n01))

        @pl.when(k == 1)
        def _():
            n02 = facing[1]
            n12 = dot_t(part(4) - dot_t(n02, facing[0]), inverse, HI).astype(BF16)
            facing[2] = n12
            load(part(5) - dot_t(n02, n02) - dot_t(n12, n12))

        return carry

    lax.fori_loop(0, STEPS, step, 0)


def factor(top):
    return pl.pallas_call(
        factor_kernel,
        out_shape=[
            jax.ShapeDtypeStruct((STEPS, B, B), F32),
            jax.ShapeDtypeStruct((STEPS, B, B), F32),
            jax.ShapeDtypeStruct((STEPS, B, B), BF16),
        ],
        in_specs=[VM],
        out_specs=[VM] * 3,
        scratch_shapes=[pltpu.VMEM((B, 2 * B), F32)],
        compiler_params=params(),
        cost_estimate=cost(15),
        name="factor",
    )(top)


def sort_kernel(pos, *refs):
    pieces, keep, give, held, sems = refs[:NQ], *refs[NQ:]
    col = pos[1]
    x, y, core = col // 8, col // 2 % 4, col % 2
    half = CH * B
    for n, k in ((0, jnp.where(core == 0, 0, 1)), (1, 2)):
        shift = x * 4 + (y - k // 2 + 4) % 4
        for s in range(NQ):

            @pl.when(shift == s)
            def _(n=n, s=s):
                pltpu.make_async_copy(pieces[s], held.at[n], sems.at[n]).start()

    for n in range(2):
        pltpu.make_async_copy(pieces[0], held.at[n], sems.at[n]).wait()
    for n in range(2):
        at = slice(n * half, (n + 1) * half)
        keep[at] = held[n, pl.ds(pl.multiple_of(core * half, half), half)]
        give[at] = held[n, pl.ds(pl.multiple_of((1 - core) * half, half), half)]


def sort(pos, pieces):
    shape = jax.ShapeDtypeStruct((2 * CH * B, B), F32)
    return pl.pallas_call(
        sort_kernel,
        out_shape=[shape, shape],
        in_specs=[SM] + [ANY] * NQ,
        out_specs=[VM, VM],
        scratch_shapes=[
            pltpu.VMEM((2, 2 * CH * B, B), F32),
            pltpu.SemaphoreType.DMA((2,)),
        ],
        compiler_params=params(),
        cost_estimate=cost(2),
        name="sort",
    )(pos, *pieces)


def panels_kernel(pos, inv, facing, keep, got, out):
    first = pos[1] % 2 == 0
    half = CH * B
    w0 = jnp.where(first, keep[:half], got[:half])
    w1 = jnp.where(first, got[:half], keep[:half])
    w2 = jnp.where(first, keep[half:], got[half:])
    n0 = dot_t(w0, inv[0], HI).astype(BF16)
    out[:, :B] = n0
    n1 = dot_t(w1 - dot_t(n0, facing[0]), inv[1], HI).astype(BF16)
    out[:, B : 2 * B] = n1
    rest = w2 - dot_t(n0, facing[1]) - dot_t(n1, facing[2])
    out[:, 2 * B :] = dot_t(rest, inv[2], HI).astype(BF16)


def panels(pos, inv, facing, keep, got):
    return pl.pallas_call(
        panels_kernel,
        out_shape=jax.ShapeDtypeStruct((CH * B, STEPS * B), BF16),
        in_specs=[SM] + [VM] * 4,
        out_specs=VM,
        compiler_params=params(),
        cost_estimate=cost(4),
        name="panels",
    )(pos, inv, facing, keep, got)


def solve_kernel(pos, work, inv, chunk, out):
    del chunk
    col = pos[1]

    @pl.when(col >= STEPS)
    def _():
        out[...] = work[...]

    @pl.when(col < STEPS)
    def _():
        inverse = inv[jnp.minimum(col, STEPS - 1)]

        def solve(b, carry):
            at = pl.ds(pl.multiple_of(b * (ROWS // NR), 8), ROWS // NR)
            out[at] = dot_t(work[at], inverse, HI)
            return carry

        lax.fori_loop(0, NR, solve, 0)


def solve(pos, work, inv, chunk):
    return pl.pallas_call(
        solve_kernel,
        out_shape=jax.ShapeDtypeStruct((ROWS, B), F32),
        in_specs=[SM, VM, VM, ANY],
        out_specs=VM,
        compiler_params=params(),
        cost_estimate=cost(20),
        name="solve",
    )(pos, work, inv, chunk)


def across_kernel(pos, face, inv, parts):
    col = pos[1]
    lane = lax.broadcasted_iota(jnp.int32, (B, STEPS * B), 1) // B
    across = jnp.where(lane < col, face[...].astype(F32), 0.0)
    parts[0] = across.astype(BF16)

    @pl.when(col < STEPS)
    def _():
        inverse = inv[jnp.minimum(col, STEPS - 1)]
        rest = lax.dot_general(
            inverse, across, (((1,), (0,)), ((), ())), precision=HI, preferred_element_type=F32
        )
        for i in range(3):
            parts[i] = rest.astype(BF16)
            rest = rest - parts[i].astype(F32)


def across(pos, face, inv):
    return pl.pallas_call(
        across_kernel,
        out_shape=jax.ShapeDtypeStruct((3, B, STEPS * B), BF16),
        in_specs=[SM, VM, VM],
        out_specs=VM,
        compiler_params=params(),
        cost_estimate=cost(1),
        name="across",
    )(pos, face, inv)


def update_kernel(flip, pos, work, panel, parts, low, out, held, ins, outs):
    row, col = pos[0], pos[1]
    core = (col + flip) % 2

    def each(q, there, act):
        owner = 2 * q + core
        sems = outs if there else ins
        for n, (first, t, end) in enumerate(((owner, 0, 1), (TOP + 3 * owner, 1, CH))):
            hbm = pl.ds(pl.multiple_of(first * B, B), (end - t) * B)
            here = held.at[q, pl.ds(t * B, (end - t) * B)]
            copy = (
                pltpu.make_async_copy(here, out.at[hbm], sems.at[q, n])
                if there
                else pltpu.make_async_copy(work.at[hbm], here, sems.at[q, n])
            )
            if t and q == NQ - 1:
                pl.when(owner < NC - 1)(lambda copy=copy: act(copy))
            else:
                act(copy)

    for q in range(NQ):
        each(q, False, lambda copy: copy.start())
    for q in range(NQ):
        owner = 2 * q + core
        rows = slice(q * CH * B, (q + 1) * CH * B)
        each(q, False, lambda copy: copy.wait())

        @pl.when(col >= STEPS)
        def _(q=q, rows=rows):
            held[q] = held[q] - dot_t(panel[rows], parts[0])

        for k in range(1, STEPS):

            @pl.when(col == k)
            def _(k=k, q=q, rows=rows):
                left = panel[rows, : k * B]
                total = dot_t(left, parts[0, :, : k * B])
                for i in range(1, 3):
                    total = total + dot_t(left, parts[i, :, : k * B])
                held[q] = held[q] - total

        @pl.when((row == 0) & (owner <= col))
        def _(q=q, owner=owner):
            r = lax.broadcasted_iota(jnp.int32, (B, B), 0)
            c = lax.broadcasted_iota(jnp.int32, (B, B), 1)
            value = jnp.where(col < STEPS, low[jnp.minimum(col, STEPS - 1)], held[q, :B])
            held[q, :B] = jnp.where((owner == col) & (r >= c), value, 0.0)

        each(q, True, lambda copy: copy.start())

    for q in range(NQ):
        each(q, True, lambda copy: copy.wait())


def update(flip, pos, work, panel, parts, low):
    return pl.pallas_call(
        functools.partial(update_kernel, flip),
        out_shape=jax.ShapeDtypeStruct((ROWS, B), F32),
        in_specs=[SM, ANY, VM, VM, VM],
        out_specs=ANY,
        input_output_aliases={1: 0},
        scratch_shapes=[
            pltpu.VMEM((NQ, CH * B, B), F32),
            pltpu.SemaphoreType.DMA((NQ, 2)),
            pltpu.SemaphoreType.DMA((NQ, 2)),
        ],
        compiler_params=params(),
        cost_estimate=cost(6),
        name="update",
    )(pos, work, panel, parts, low)


def send(x, pairs):
    return lax.ppermute(x, ("row", "col"), [(a * NC + b, c * NC + d) for (a, b), (c, d) in pairs])


def spread_top(front, row, col):
    parts = [front[k * B : STEPS * B] for k in range(STEPS)]
    second = send(parts[1], [((0, 1), (0, 0))])
    third = send(parts[2], [((0, 2), (0, 0))])
    root = (row == 0) & (col == 0)
    top = jnp.where(root, jnp.concatenate([parts[0], second, third]), 0.0)

    def hop(top, *moves):
        return sum([send(top, pairs) for pairs in moves], top)

    even = range(0, NC, 2)
    targets = (2, 6, 8, 4)
    top = hop(top, *[[((0, 0), (0, c))] for c in targets])
    top = hop(top, [((0, c), (0, c + 8)) for c in (2, 4, 6)])
    top = hop(top, [((0, c), (1, c)) for c in even])
    pair = [(r, c) for r in range(2) for c in even]
    top = hop(top, [((r, c), (r + 2, c)) for r, c in pair], [((r, c), (r + 6, c)) for r, c in pair])
    top = hop(top, [((r + 2, c), (r + 4, c)) for r, c in pair])
    return hop(top, [((r, c), (r, c + 1)) for c in even for r in range(NR)])


def on_device(front, child_update, child_rows):
    row, col = lax.axis_index("row"), lax.axis_index("col")
    pos = jnp.stack([row, col]).astype(jnp.int32)
    packed = pack(pos, child_rows, child_update)
    got = lax.all_to_all(packed, "row", 0, 0, tiled=True)
    top = spread_top(front, row, col)
    low, inv, facing = factor(top)
    work, *chunks = assemble(pos, child_rows, front, got)

    def outward(s):
        pairs = []
        for k in range(STEPS):
            pairs.append((k, s // 4 * 8 + (k // 2 + s) % 4 * 2 + k % 2))
        return lax.ppermute(chunks[s], "col", pairs)

    def home(k, dx, dy):
        return dx * 8 + (k // 2 + dy) % 4 * 2 + k % 2

    pieces = {0: chunks[0]}
    relayed = lax.ppermute(chunks[7], "col", [(k, home(k, 0, 3)) for k in range(STEPS)])
    order = (1, 4, 2, 5, 3, 6)
    for s in order:
        pieces[s] = outward(s)
    pieces[7] = lax.ppermute(relayed, "col", [(home(k, 0, 3), home(k, 1, 3)) for k in range(STEPS)])
    keep, give = sort(pos, [pieces[s] for s in range(NQ)])
    flip = [(c, c ^ 1) for c in range(NC)]
    chunk = panels(pos, inv, facing, keep, lax.ppermute(give, "col", flip))
    cores = [[c for c in range(NC) if c % 2 == p] for p in range(2)]
    mine = lax.all_to_all(
        jnp.tile(chunk, (NQ, 1)), "col", 0, 0, axis_index_groups=cores, tiled=True
    )
    face = jnp.where(row == 0, chunk[:B], jnp.zeros_like(chunk[:B]))

    def hop(face, *moves):
        return sum([lax.ppermute(face, "row", pairs) for pairs in moves], face)

    face = hop(face, [(0, 2)], [(0, 6)])
    face = hop(face, [(2, 4)])
    face = hop(face, [(0, 1), (2, 3), (4, 5), (6, 7)])
    parts = across(pos, face, inv)
    work = solve(pos, work, inv, chunk)
    work = update(0, pos, work, mine, parts, low)
    other = lax.ppermute(mine, "col", flip)
    return update(1, pos, work, other, parts, low)


def solution(mesh):
    in_specs = (P("row", "col"), P("row", "col"), P())
    return jax.shard_map(
        on_device, mesh=mesh, in_specs=in_specs, out_specs=P("row", "col"), check_vma=False
    )
```

time: 1340 us -> 220 us (0.16)
  the two profiles are of different devices: /device:TPU:0 before, /device:TPU:72 now
where the time goes in v1:
time: 220 us; the launch traced here: 219 us
  Pallas kernels  58.9 us (27%)
  blocking collectives  58.5 us (27%)
  waiting for transfers between devices  48.4 us (22%)
  starting transfers between devices  40 us (18%)
  local copies, waits for them, and re-layouts  8.77 us (4%)
  other arithmetic  3.54 us (2%)
    all_to_all x1, blocking collectives, on_device(): lax.all_to_all(jnp.tile(chunk, (NQ, 1)), 'col', 0, 0, axis_index_groups=c...  58.5 us
    all_to_all x1, waiting for transfers between devices, on_device(): got = lax.all_to_all(packed, 'row', 0, 0, tiled=True)  18.5 us
    pallas_call x1, Pallas kernels, factor(): pl.pallas_call(factor_kernel, out_shape=[jax.ShapeDtypeStruct((STEPS, B,...  14.9 us
    ppermute x6, starting transfers between devices, outward(): return lax.ppermute(chunks[s], 'col', pairs)  14.4 us
    ppermute x6, waiting for transfers between devices, outward(): return lax.ppermute(chunks[s], 'col', pairs)  14.3 us
    pallas_call x2, Pallas kernels, update(): pl.pallas_call(functools.partial(update_kernel, flip), out_shape=jax.Shap...  14 us
    ppermute x12, starting transfers between devices, send(): lax.ppermute(x, ('row', 'col'), [(a * NC + b, c * NC + d) for (a, b), (c,...  10.9 us
    pallas_call x1, Pallas kernels, solve(): pl.pallas_call(solve_kernel, out_shape=jax.ShapeDtypeStruct((ROWS, B), F3...  8.68 us
  transfers between devices with their start and end apart: 27, of which 6 were waited for; matrix products, arithmetic and copies ran while one was open for 2% of the time, Pallas kernels for 21%

profile of v1, /device:TPU:72, one launch (start us, length us, event | category | flops | bytes accessed | tf_op | source)
XLA Modules:
  0.0 218.8 jit_solution(1902414427629078550)
XLA Ops:
  0.0 0.9 slice.13
  0.9 0.7 collective-permute-start
  1.6 0.8 slice.14
  3.1 0.9 slice.12
  4.1 0.7 collective-permute-start.5
  4.8 0.7 collective-permute-start.4
  5.5 1.4 collective-permute-start.3
  6.9 1.4 collective-permute-start.2
  8.9 4.1 %pack.1 = bf16[8192,128]{1,0:T(8,128)(2,1)} custom-call(s32[2]{0:T(128)} %pad_add_fusion.pos, s32[4,244]{1,0:T(4,128)} %rows.3, bf16[7808,128]{1,0:T(8,128)(2,1)} %child.1), custom_call_target="tpu_custom_call" | custom-call | flops 2700000000 | bytes 9000000 | tf_op jit(solution)/shard_map/pack/pallas_call | solution.py:68
  13.1 6.2 %all-to-all-start = ((bf16[8,1024,128]{2,1,0:T(8,128)(2,1)}), bf16[8,1024,128]{2,1,0:T(8,128)(2,1)S(1)}, u32[]{:S(2)}, u32[]{:S(2)}) async-start(bf16[8,1024,128]{2,1,0:T(8,128)(2,1)} %bitcast.8), calls=%async_computation | async-start | bytes 4194304 | tf_op jit(solution)/shard_map/all_to_all | solution.py:450
  19.3 1.2 add_add_fusion.1
  20.5 0.7 collective-permute-start.6
  21.3 0.7 collective-permute-start.7
  22.0 0.7 collective-permute-start.9
  22.7 0.7 collective-permute-start.8
  23.5 1.3 collective-permute-start.10
  24.8 18.5 %all-to-all-done = bf16[8,1024,128]{2,1,0:T(8,128)(2,1)S(1)} async-done(((bf16[8,1024,128]{2,1,0:T(8,128)(2,1)}), bf16[8,1024,128]{2,1,0:T(8,128)(2,1)S(1)}, u32[]{:S(2)}, u32[]{:S(2)}) %all-to-all-start) | async-done | bytes 2097184 | tf_op jit(solution)/shard_map/all_to_all | solution.py:450
  43.3 1.3 copy-done.1
  44.6 8.3 %assemble.1 = (f32[7808,128]{1,0:T(8,128)}, f32[1024,128]{1,0:T(8,128)}, f32[1024,128]{1,0:T(8,128)}, f32[1024,128]{1,0:T(8,128)}, f32[1024,128]{1,0:T(8,128)}, ...) custom-call(s32[2]{0:T(128)} %pad_add_fusion.pos, s32[4,244]{1,0:T(4,128)} %rows.3, ...), custom_call_target="tpu_custom_call" | custom-call | flops 5400000000 | bytes 18000000 | tf_op jit(solution)/shard_map/assemble/pallas_call | solution.py:115
  52.9 3.2 %collective-permute-start.12 = (f32[1024,128]{1,0:T(8,128)}, f32[1024,128]{1,0:T(8,128)S(1)}, u32[]{:S(2)}, u32[]{:S(2)}) collective-permute-start(f32[1024,128]{1,0:T(8,128)} %get-tuple-element.23), channel_id=1, source_target_pairs={{0,2},{1,3},{2,4},{16,18},{17,19},{18,20},{32,34},{33,35},{34,36},... | collective-permute-start | bytes 1572872 | tf_op jit(solution)/shard_map/ppermute | solution.py:459
  56.1 1.4 collective-permute-start.13
  57.6 3.9 %collective-permute-start.18 = (f32[1024,128]{1,0:T(8,128)}, f32[1024,128]{1,0:T(8,128)S(1)}, u32[]{:S(2)}, u32[]{:S(2)}) collective-permute-start(f32[1024,128]{1,0:T(8,128)} %get-tuple-element.29), channel_id=1, source_target_pairs={{0,6},{1,7},{2,0},{16,22},{17,23},{18,16},{32,38},{33,39},{34,32},... | collective-permute-start | bytes 1572872 | tf_op jit(solution)/shard_map/ppermute | solution.py:465
  61.5 7.3 %collective-permute-done.10 = f32[768,128]{1,0:T(8,128)S(1)} collective-permute-done((f32[768,128]{1,0:T(8,128)S(1)}, f32[768,128]{1,0:T(8,128)S(1)}, u32[]{:S(2)}, u32[]{:S(2)}) %collective-permute-start.10) | collective-permute-done | bytes 393248 | tf_op jit(solution)/shard_map/ppermute | solution.py:422
  68.8 1.3 collective-permute-start.11
  70.1 1.3 collective-permute-start.14
  71.5 5.3 %collective-permute-start.15 = (f32[1024,128]{1,0:T(8,128)}, f32[1024,128]{1,0:T(8,128)S(1)}, u32[]{:S(2)}, u32[]{:S(2)}) collective-permute-start(f32[1024,128]{1,0:T(8,128)} %get-tuple-element.26), channel_id=1, source_target_pairs={{0,8},{1,9},{2,10},{16,24},{17,25},{18,26},{32,40},{33,41},{34,42}... | collective-permute-start | bytes 1572872 | tf_op jit(solution)/shard_map/ppermute | solution.py:459
  76.8 1.7 collective-permute-start.16
  78.5 1.4 collective-permute-start.17
  80.0 0.7 collective-permute-start.19
  80.7 0.8 add.51.top
  81.5 2.3 %collective-permute-done.15.refs_4_ = f32[1024,128]{1,0:T(8,128)S(1)} collective-permute-done((f32[1024,128]{1,0:T(8,128)}, f32[1024,128]{1,0:T(8,128)S(1)}, u32[]{:S(2)}, u32[]{:S(2)}) %collective-permute-start.15) | collective-permute-done | bytes 524320 | tf_op jit(solution)/shard_map/ppermute | solution.py:459
  83.7 5.8 %collective-permute-done.16.refs_5_ = f32[1024,128]{1,0:T(8,128)S(1)} collective-permute-done((f32[1024,128]{1,0:T(8,128)}, f32[1024,128]{1,0:T(8,128)S(1)}, u32[]{:S(2)}, u32[]{:S(2)}) %collective-permute-start.16) | collective-permute-done | bytes 524320 | tf_op jit(solution)/shard_map/ppermute | solution.py:459
  89.6 6.2 %collective-permute-done.17.refs_6_ = f32[1024,128]{1,0:T(8,128)S(1)} collective-permute-done((f32[1024,128]{1,0:T(8,128)}, f32[1024,128]{1,0:T(8,128)S(1)}, u32[]{:S(2)}, u32[]{:S(2)}) %collective-permute-start.17) | collective-permute-done | bytes 524320 | tf_op jit(solution)/shard_map/ppermute | solution.py:459
  95.8 0.8 copy-done.9
  96.8 3.0 %sort.1 = (f32[1024,128]{1,0:T(8,128)}, f32[1024,128]{1,0:T(8,128)}) custom-call(s32[2]{0:T(128)} %pad_add_fusion.pos, f32[1024,128]{1,0:T(8,128)} %get-tuple-element.22.refs_0_, f32[1024,128]{1,0:T(8,128)} %copy-done.4, f32[1024,128]{1,0:T(8,128)} %copy-done.5, f32[1024,128]{1,0:T(8,128)} %copy-done.6, f32[1024,128]{1,0:T(8,128)} %copy-done.7, ...), custom_call_target="tpu_custom_call" | custom-call | flops 1800000000 | bytes 6000000 | tf_op jit(solution)/shard_map/sort/pallas_call | solution.py:247
  99.9 14.9 %factor.1 = (f32[3,128,128]{2,1,0:T(8,128)}, f32[3,128,128]{2,1,0:T(8,128)}, bf16[3,128,128]{2,1,0:T(8,128)(2,1)}) custom-call(f32[768,128]{1,0:T(8,128)} %add.51.top), custom_call_target="tpu_custom_call" | custom-call | flops 13500000256 | bytes 45000000 | tf_op jit(solution)/shard_map/factor/pallas_call | solution.py:208
  114.7 0.8 copy-done.11
  115.5 3.8 %panels.1.chunk = bf16[512,384]{1,0:T(8,128)(2,1)} custom-call(s32[2]{0:T(128)} %pad_add_fusion.pos, f32[3,128,128]{2,1,0:T(8,128)} %get-tuple-element.20.inv, bf16[3,128,128]{2,1,0:T(8,128)(2,1)} %get-tuple-element.21.facing, f32[1024,128]{1,0:T(8,128)} %get-tuple-element.30.keep, f32[1024,128]{1,0:T(8,128)} %copy-done.11), custom_call_target="tpu_custom_call" | custom-call | flops 3600000000 | bytes 12000000 | tf_op jit(solution)/shard_map/panels/pallas_call | solution.py:277
  119.3 1.3 tile.2
  120.6 58.5 %all_to_all.19 = bf16[8,512,384]{2,1,0:T(8,128)(2,1)S(1)} all-to-all(bf16[8,512,384]{2,1,0:T(8,128)(2,1)S(1)} %tile.2), channel_id=1, replica_groups={{0,2,4,6,8,10,12,14},{1,3,5,7,9,11,13,15},{16,18,20,22,24,26,28,30},{17..., dimensions={0} | all-to-all | bytes 6291456 | tf_op jit(solution)/shard_map/all_to_all | solution.py:474
  180.5 1.3 collective-permute-start.23
  181.8 8.3 %collective-permute-done.23 = bf16[128,384]{1,0:T(8,128)(2,1)S(1)} collective-permute-done((bf16[128,384]{1,0:T(8,128)(2,1)S(1)}, bf16[128,384]{1,0:T(8,128)(2,1)S(1)}, u32[]{:S(2)}, u32[]{:S(2)}) %collective-permute-start.23) | collective-permute-done | bytes 98336 | tf_op jit(solution)/shard_map/ppermute | solution.py:480
  190.2 1.3 collective-permute-start.24
  191.5 8.7 %solve.1.work = f32[7808,128]{1,0:T(8,128)} custom-call(s32[2]{0:T(128)} %pad_add_fusion.pos, f32[7808,128]{1,0:T(8,128)} %get-tuple-element.19.work, f32[3,128,128]{2,1,0:T(8,128)} %get-tuple-element.20.inv, bf16[512,384]{1,0:T(8,128)(2,1)} %panels.1.chunk), custom_call_target="tpu_custom_call" | custom-call | flops 17999998976 | bytes 60000000 | tf_op jit(solution)/shard_map/solve/pallas_call | solution.py:309
  200.8 2.1 across.1.parts
  202.9 7.1 %update.2.work = f32[7808,128]{1,0:T(8,128)} custom-call(s32[2]{0:T(128)} %pad_add_fusion.pos, f32[7808,128]{1,0:T(8,128)} %solve.1.work, bf16[4096,384]{1,0:T(8,128)(2,1)} %bitcast.6, bf16[3,128,384]{2,1,0:T(8,128)(2,1)} %across.1.parts, f32[3,128,128]{2,1,0:T(8,128)} %get-tuple-element.32.low), custom_call_target="tpu_custom_call", output_to_operand_aliasing={{}: (1, {})} | custom-call | flops 5400000000 | bytes 18000000 | tf_op jit(solution)/shard_map/update/pallas_call | solution.py:404
  210.1 1.6 copy-done.3
  211.7 6.9 %update.3 = f32[7808,128]{1,0:T(8,128)} custom-call(s32[2]{0:T(128)} %pad_add_fusion.pos, f32[7808,128]{1,0:T(8,128)} %update.2.work, bf16[4096,384]{1,0:T(8,128)(2,1)} %copy-done.3, bf16[3,128,384]{2,1,0:T(8,128)(2,1)} %across.1.parts, f32[3,128,128]{2,1,0:T(8,128)} %get-tuple-element.32.low), custom_call_target="tpu_custom_call", output_to_operand_aliasing={{}: (1, {})} | custom-call | flops 5400000000 | bytes 18000000 | tf_op jit(solution)/shard_map/update/pallas_call | solution.py:404
  (56 shorter events, 3.9 us)
Async XLA Ops:
  0.9 3.2 %collective-permute-start = (f32[256,128]{1,0:T(8,128)S(1)}, f32[256,128]{1,0:T(8,128)S(1)}, u32[]{:S(2)}, u32[]{:S(2)}) collective-permute-start(f32[256,128]{1,0:T(8,128)S(1)} %slice.13), channel_id=1, source_target_pairs={{1,0}} | collective-permute-start | bytes 393224 | tf_op jit(solution)/shard_map/ppermute | solution.py:422
  2.4 1.6 collective-permute-start.1
  4.1 15.1 %collective-permute-start.5 = (f32[768,128]{1,0:T(8,128)S(1)}, f32[768,128]{1,0:T(8,128)S(1)}, u32[]{:S(2)}, u32[]{:S(2)}) collective-permute-start(f32[768,128]{1,0:T(8,128)S(1)} %maximum_select_fusion), channel_id=1, source_target_pairs={{0,4}} | collective-permute-start | bytes 1179656 | tf_op jit(solution)/shard_map/ppermute | solution.py:422
  4.8 14.4 %collective-permute-start.4 = (f32[768,128]{1,0:T(8,128)S(1)}, f32[768,128]{1,0:T(8,128)S(1)}, u32[]{:S(2)}, u32[]{:S(2)}) collective-permute-start(f32[768,128]{1,0:T(8,128)S(1)} %maximum_select_fusion), channel_id=1, source_target_pairs={{0,8}} | collective-permute-start | bytes 1179656 | tf_op jit(solution)/shard_map/ppermute | solution.py:422
  5.5 13.8 %collective-permute-start.3 = (f32[768,128]{1,0:T(8,128)S(1)}, f32[768,128]{1,0:T(8,128)}, u32[]{:S(2)}, u32[]{:S(2)}) collective-permute-start(f32[768,128]{1,0:T(8,128)S(1)} %maximum_select_fusion), channel_id=1, source_target_pairs={{0,6}} | collective-permute-start | bytes 1179656 | tf_op jit(solution)/shard_map/ppermute | solution.py:422
  6.9 12.4 %collective-permute-start.2 = (f32[768,128]{1,0:T(8,128)S(1)}, f32[768,128]{1,0:T(8,128)}, u32[]{:S(2)}, u32[]{:S(2)}) collective-permute-start(f32[768,128]{1,0:T(8,128)S(1)} %maximum_select_fusion), channel_id=1, source_target_pairs={{0,2}} | collective-permute-start | bytes 1179656 | tf_op jit(solution)/shard_map/ppermute | solution.py:422
  13.1 30.2 %all-to-all-start = ((bf16[8,1024,128]{2,1,0:T(8,128)(2,1)}), bf16[8,1024,128]{2,1,0:T(8,128)(2,1)S(1)}, u32[]{:S(2)}, u32[]{:S(2)}) async-start(bf16[8,1024,128]{2,1,0:T(8,128)(2,1)} %bitcast.8), calls=%async_computation | async-start | bytes 4194304 | tf_op jit(solution)/shard_map/all_to_all | solution.py:450
  20.5 0.7 collective-permute-start.6
  21.3 0.7 collective-permute-start.7
  22.0 1.4 collective-permute-start.9
  22.7 0.7 collective-permute-start.8
  23.5 45.3 %collective-permute-start.10 = (f32[768,128]{1,0:T(8,128)S(1)}, f32[768,128]{1,0:T(8,128)S(1)}, u32[]{:S(2)}, u32[]{:S(2)}) collective-permute-start(f32[768,128]{1,0:T(8,128)S(1)} %add_add_fusion), channel_id=1, source_target_pairs={{32,64},{34,66},{36,68},{38,70},{40,72},{42,74},{44,76},{46,78},{4... | collective-permute-start | bytes 1179656 | tf_op jit(solution)/shard_map/ppermute | solution.py:422
  43.3 1.3 copy-start.1
  52.9 18.5 %collective-permute-start.12 = (f32[1024,128]{1,0:T(8,128)}, f32[1024,128]{1,0:T(8,128)S(1)}, u32[]{:S(2)}, u32[]{:S(2)}) collective-permute-start(f32[1024,128]{1,0:T(8,128)} %get-tuple-element.23), channel_id=1, source_target_pairs={{0,2},{1,3},{2,4},{16,18},{17,19},{18,20},{32,34},{33,35},{34,36},... | collective-permute-start | bytes 1572872 | tf_op jit(solution)/shard_map/ppermute | solution.py:459
  56.1 20.6 %collective-permute-start.13 = (f32[1024,128]{1,0:T(8,128)}, f32[1024,128]{1,0:T(8,128)S(1)}, u32[]{:S(2)}, u32[]{:S(2)}) collective-permute-start(f32[1024,128]{1,0:T(8,128)} %get-tuple-element.24), channel_id=1, source_target_pairs={{0,4},{1,5},{2,6},{16,20},{17,21},{18,22},{32,36},{33,37},{34,38},... | collective-permute-start | bytes 1572872 | tf_op jit(solution)/shard_map/ppermute | solution.py:459
  57.6 21.0 %collective-permute-start.18 = (f32[1024,128]{1,0:T(8,128)}, f32[1024,128]{1,0:T(8,128)S(1)}, u32[]{:S(2)}, u32[]{:S(2)}) collective-permute-start(f32[1024,128]{1,0:T(8,128)} %get-tuple-element.29), channel_id=1, source_target_pairs={{0,6},{1,7},{2,0},{16,22},{17,23},{18,16},{32,38},{33,39},{34,32},... | collective-permute-start | bytes 1572872 | tf_op jit(solution)/shard_map/ppermute | solution.py:465
  68.8 11.2 %collective-permute-start.11 = (f32[768,128]{1,0:T(8,128)S(1)}, f32[768,128]{1,0:T(8,128)S(1)}, u32[]{:S(2)}, u32[]{:S(2)}) collective-permute-start(f32[768,128]{1,0:T(8,128)S(1)} %add.50), channel_id=1, source_target_pairs={{0,1},{16,17},{32,33},{48,49},{64,65},{80,81},{96,97},{112,113},{2... | collective-permute-start | bytes 1179656 | tf_op jit(solution)/shard_map/ppermute | solution.py:422
  70.1 11.4 %collective-permute-start.14 = (f32[1024,128]{1,0:T(8,128)}, f32[1024,128]{1,0:T(8,128)S(1)}, u32[]{:S(2)}, u32[]{:S(2)}) collective-permute-start(f32[1024,128]{1,0:T(8,128)} %get-tuple-element.25), channel_id=1, source_target_pairs={{0,6},{1,7},{2,0},{16,22},{17,23},{18,16},{32,38},{33,39},{34,32},... | collective-permute-start | bytes 1572872 | tf_op jit(solution)/shard_map/ppermute | solution.py:459
  71.5 24.3 %copy-start.4 = (f32[1024,128]{1,0:T(8,128)}, f32[1024,128]{1,0:T(8,128)S(1)}, u32[]{:S(2)}) copy-start(f32[1024,128]{1,0:T(8,128)S(1)} %collective-permute-done.12.refs_1_) | copy-start | bytes 1572868
  71.5 12.3 %collective-permute-start.15 = (f32[1024,128]{1,0:T(8,128)}, f32[1024,128]{1,0:T(8,128)S(1)}, u32[]{:S(2)}, u32[]{:S(2)}) collective-permute-start(f32[1024,128]{1,0:T(8,128)} %get-tuple-element.26), channel_id=1, source_target_pairs={{0,8},{1,9},{2,10},{16,24},{17,25},{18,26},{32,40},{33,41},{34,42}... | collective-permute-start | bytes 1572872 | tf_op jit(solution)/shard_map/ppermute | solution.py:459
  76.8 19.0 %copy-start.5 = (f32[1024,128]{1,0:T(8,128)}, f32[1024,128]{1,0:T(8,128)S(1)}, u32[]{:S(2)}) copy-start(f32[1024,128]{1,0:T(8,128)S(1)} %collective-permute-done.13.refs_2_) | copy-start | bytes 1572868
  76.8 12.8 %collective-permute-start.16 = (f32[1024,128]{1,0:T(8,128)}, f32[1024,128]{1,0:T(8,128)S(1)}, u32[]{:S(2)}, u32[]{:S(2)}) collective-permute-start(f32[1024,128]{1,0:T(8,128)} %get-tuple-element.27), channel_id=1, source_target_pairs={{0,10},{1,11},{2,12},{16,26},{17,27},{18,28},{32,42},{33,43},{34,4... | collective-permute-start | bytes 1572872 | tf_op jit(solution)/shard_map/ppermute | solution.py:459
  78.5 17.2 %collective-permute-start.17 = (f32[1024,128]{1,0:T(8,128)}, f32[1024,128]{1,0:T(8,128)S(1)}, u32[]{:S(2)}, u32[]{:S(2)}) collective-permute-start(f32[1024,128]{1,0:T(8,128)} %get-tuple-element.28), channel_id=1, source_target_pairs={{0,12},{1,13},{2,14},{16,28},{17,29},{18,30},{32,44},{33,45},{34,4... | collective-permute-start | bytes 1572872 | tf_op jit(solution)/shard_map/ppermute | solution.py:459
  80.0 15.8 %collective-permute-start.19 = (f32[1024,128]{1,0:T(8,128)S(1)}, f32[1024,128]{1,0:T(8,128)S(1)}, u32[]{:S(2)}, u32[]{:S(2)}) collective-permute-start(f32[1024,128]{1,0:T(8,128)S(1)} %collective-permute-done.18), channel_id=1, source_target_pairs={{6,14},{7,15},{0,8},{22,30},{23,31},{16,24},{38,46},{39,47},{32,40... | collective-permute-start | bytes 1572872 | tf_op jit(solution)/shard_map/ppermute | solution.py:469
  81.5 14.3 %copy-start.6 = (f32[1024,128]{1,0:T(8,128)}, f32[1024,128]{1,0:T(8,128)S(1)}, u32[]{:S(2)}) copy-start(f32[1024,128]{1,0:T(8,128)S(1)} %collective-permute-done.14.refs_3_) | copy-start | bytes 1572868
  83.7 12.0 %copy-start.7 = (f32[1024,128]{1,0:T(8,128)}, f32[1024,128]{1,0:T(8,128)S(1)}, u32[]{:S(2)}) copy-start(f32[1024,128]{1,0:T(8,128)S(1)} %collective-permute-done.15.refs_4_) | copy-start | bytes 1572868
  89.6 6.2 %copy-start.8 = (f32[1024,128]{1,0:T(8,128)}, f32[1024,128]{1,0:T(8,128)S(1)}, u32[]{:S(2)}) copy-start(f32[1024,128]{1,0:T(8,128)S(1)} %collective-permute-done.16.refs_5_) | copy-start | bytes 1572868
  95.7 0.9 copy-start.9
  95.7 1.1 copy-start.10
  99.8 15.0 %collective-permute-start.20 = (f32[1024,128]{1,0:T(8,128)}, f32[1024,128]{1,0:T(8,128)S(1)}, u32[]{:S(2)}, u32[]{:S(2)}) collective-permute-start(f32[1024,128]{1,0:T(8,128)} %get-tuple-element.31), channel_id=1, source_target_pairs={{0,1},{1,0},{2,3},{3,2},{4,5},{5,4},{6,7},{7,6},{8,9},{9,8},{10,11... | collective-permute-start | bytes 1572872 | tf_op jit(solution)/shard_map/ppermute | solution.py:472
  114.7 0.8 copy-start.11
  120.5 58.5 %copy-start.2 = (bf16[512,384]{1,0:T(8,128)(2,1)S(1)}, bf16[512,384]{1,0:T(8,128)(2,1)}, u32[]{:S(2)}) copy-start(bf16[512,384]{1,0:T(8,128)(2,1)} %panels.1.chunk) | copy-start | bytes 1179652
  179.1 21.1 %copy-start = (bf16[8,512,384]{2,1,0:T(8,128)(2,1)}, bf16[8,512,384]{2,1,0:T(8,128)(2,1)S(1)}, u32[]{:S(2)}) copy-start(bf16[8,512,384]{2,1,0:T(8,128)(2,1)S(1)} %all_to_all.19) | copy-start | bytes 9437188
  179.1 31.0 %collective-permute-start.25 = (bf16[4096,384]{1,0:T(8,128)(2,1)S(1)}, bf16[4096,384]{1,0:T(8,128)(2,1)S(1)}, u32[]{:S(2)}, u32[]{:S(2)}) collective-permute-start(bf16[4096,384]{1,0:T(8,128)(2,1)S(1)} %bitcast.5), channel_id=1, source_target_pairs={{0,1},{1,0},{2,3},{3,2},{4,5},{5,4},{6,7},{7,6},{8,9},{9,8},{10,11... | collective-permute-start | bytes 9437192 | tf_op jit(solution)/shard_map/ppermute | solution.py:488
  179.1 1.4 collective-permute-start.22
  179.8 0.7 collective-permute-start.21
  180.5 9.6 %collective-permute-start.23 = (bf16[128,384]{1,0:T(8,128)(2,1)S(1)}, bf16[128,384]{1,0:T(8,128)(2,1)S(1)}, u32[]{:S(2)}, u32[]{:S(2)}) collective-permute-start(bf16[128,384]{1,0:T(8,128)(2,1)S(1)} %add_add_fusion.2), channel_id=1, source_target_pairs={{32,64},{33,65},{34,66},{35,67},{36,68},{37,69},{38,70},{39,71},{4... | collective-permute-start | bytes 294920 | tf_op jit(solution)/shard_map/ppermute | solution.py:480
  190.2 10.0 %collective-permute-start.24 = (bf16[128,384]{1,0:T(8,128)(2,1)S(1)}, bf16[128,384]{1,0:T(8,128)(2,1)S(1)}, u32[]{:S(2)}, u32[]{:S(2)}) collective-permute-start(bf16[128,384]{1,0:T(8,128)(2,1)S(1)} %add.54), channel_id=1, source_target_pairs={{0,16},{32,48},{64,80},{96,112},{1,17},{33,49},{65,81},{97,113},{2... | collective-permute-start | bytes 294920 | tf_op jit(solution)/shard_map/ppermute | solution.py:480
  210.1 1.6 copy-start.3

commit v2 on v1

--- a/solution.py
+++ b/solution.py
@@ -17,6 +17,7 @@
 TOP = NC
 CH = 4
 NQ = NC // 2
+SPLIT = 5
 F32 = jnp.float32
 BF16 = jnp.bfloat16
 HI = lax.Precision.HIGHEST
@@ -25,7 +26,7 @@
 ANY = pl.BlockSpec(memory_space=pl.ANY)
 
 
-def params(mib=56):
+def params(mib):
     return pltpu.CompilerParams(vmem_limit_bytes=mib * 1024 * 1024)
 
 
@@ -37,10 +38,6 @@
     return lax.dot_general(
         a, b, (((1,), (1,)), ((), ())), precision=precision, preferred_element_type=F32
     )
-
-
-def chunk_block(owner, t):
-    return owner if t == 0 else TOP + 3 * owner + t - 1
 
 
 def pack_kernel(pos, rows, child, out, sems):
@@ -71,54 +68,102 @@
         in_specs=[SM, SM, ANY],
         out_specs=VM,
         scratch_shapes=[pltpu.SemaphoreType.DMA((NR * NR,))],
-        compiler_params=params(),
+        compiler_params=params(56),
         cost_estimate=cost(3),
         name="pack",
     )(pos, rows, child)
 
 
-def assemble_kernel(pos, rows, front, got, work, *chunks):
+def assemble_kernel(pos, rows, front, got, work, *refs):
+    chunks, (slab, child, load, arrive, store, send) = refs[: NQ + 1], refs[NQ + 1 :]
     row, col = pos[0], pos[1]
     half = col // (NC // 2)
-    work[...] = front[...]
+    part, group = ROWS // NR, NR * B
+
+    def pieces(there):
+        for i in range(NR):
+            at = pl.ds(i * part, part)
+            if there:
+                yield pltpu.make_async_copy(slab.at[at], work.at[at], store.at[i])
+            else:
+                yield pltpu.make_async_copy(front.at[at], slab.at[at], load.at[i])
+
+    arrivals = [
+        pltpu.make_async_copy(
+            got.at[pl.ds(i * group, group)], child.at[pl.ds(i * group, group)], arrive.at[i]
+        )
+        for i in range(NR)
+    ]
+    for copy in pieces(False):
+        copy.start()
+    for copy in arrivals:
+        copy.start()
+    for copy in pieces(False):
+        copy.wait()
     for src in range(NR):
+        arrivals[src].wait()
         c, g = 2 * (src // (NR // 2)) + half, src % (NR // 2)
         first = rows[c, g * RB] // RB
         residue = (row - first + NR) % NR
 
-        def add(s, carry, src=src, c=c, g=g, residue=residue):
+        def add(s, src=src, c=c, g=g, residue=residue):
             p = NR * s + residue
-
-            @pl.when(p < RB)
-            def _():
-                b = rows[c, g * RB + jnp.minimum(p, RB - 1)] - row * RB
-                at = pl.ds(pl.multiple_of(b * B, B), B)
-                piece = got[pl.ds(pl.multiple_of((src * NR + s) * B, B), B)]
-                work[at] = work[at] + piece.astype(F32)
-
-            return carry
-
-        lax.fori_loop(0, NR, add, 0)
-
-    @pl.when(col < STEPS)
-    def _():
+            b = rows[c, g * RB + jnp.minimum(p, RB - 1)] - row * RB
+            at = pl.ds(pl.multiple_of(b * B, B), B)
+            start = (src * NR + s) * B
+            slab[at] = slab[at] + child[start : start + B].astype(F32)
+
+        for s in range(NR - 1):
+            add(s)
+        pl.when(NR * (NR - 1) + residue < RB)(functools.partial(add, NR - 1))
+
+    def messages():
         for s in range(NQ):
             chip = (col // 8 + s // 4) % 2 * 4 + (col // 2 + s) % 4
             for c in range(2):
-                for t in range(CH):
-                    b = jnp.minimum(chunk_block(2 * chip + c, t), RB - 1)
-                    at = (c * CH + t) * B
-                    chunks[s][at : at + B] = work[pl.ds(pl.multiple_of(b * B, B), B)]
+                owner = 2 * chip + c
+                body = jnp.minimum(TOP + 3 * owner, RB - 3)
+                target, base = (chunks[s], c * CH) if s != SPLIT else (chunks[s + c * (NQ - s)], 0)
+                for n, (b, t, end) in enumerate(((owner, 0, 1), (body, 1, CH))):
+                    yield pltpu.make_async_copy(
+                        slab.at[pl.ds(pl.multiple_of(b * B, B), (end - t) * B)],
+                        target.at[pl.ds((base + t) * B, (end - t) * B)],
+                        send.at[s, c, n],
+                    )
+
+    @pl.when(col < STEPS)
+    def _():
+        for copy in messages():
+            copy.start()
+
+    for copy in pieces(True):
+        copy.start()
+
+    @pl.when(col < STEPS)
+    def _():
+        for copy in messages():
+            copy.wait()
+
+    for copy in pieces(True):
+        copy.wait()
 
 
 def assemble(pos, rows, front, got):
     return pl.pallas_call(
         assemble_kernel,
         out_shape=[jax.ShapeDtypeStruct((ROWS, B), F32)]
-        + [jax.ShapeDtypeStruct((2 * CH * B, B), F32)] * NQ,
-        in_specs=[SM, SM, VM, VM],
-        out_specs=[VM] * (NQ + 1),
-        compiler_params=params(),
+        + [jax.ShapeDtypeStruct(((1 + (s not in (SPLIT, NQ))) * CH * B, B), F32) for s in range(NQ + 1)],
+        in_specs=[SM, SM, ANY, ANY],
+        out_specs=[ANY] * (NQ + 2),
+        scratch_shapes=[
+            pltpu.VMEM((ROWS, B), F32),
+            pltpu.VMEM((NR * NR * B, B), BF16),
+            pltpu.SemaphoreType.DMA((NR,)),
+            pltpu.SemaphoreType.DMA((NR,)),
+            pltpu.SemaphoreType.DMA((NR,)),
+            pltpu.SemaphoreType.DMA((NQ, 2, 2)),
+        ],
+        compiler_params=params(61),
         cost_estimate=cost(6),
         name="assemble",
     )(pos, rows, front, got)
@@ -215,31 +260,45 @@
         in_specs=[VM],
         out_specs=[VM] * 3,
         scratch_shapes=[pltpu.VMEM((B, 2 * B), F32)],
-        compiler_params=params(),
+        compiler_params=params(5),
         cost_estimate=cost(15),
         name="factor",
     )(top)
 
 
 def sort_kernel(pos, *refs):
-    pieces, keep, give, held, sems = refs[:NQ], *refs[NQ:]
+    pieces, (other, direct, keep, give, sems) = refs[:NQ], refs[NQ:]
     col = pos[1]
     x, y, core = col // 8, col // 2 % 4, col % 2
     half = CH * B
+
+    def copies(n, sources):
+        for i, (out, source) in enumerate(zip((keep, give), sources, strict=True)):
+            yield pltpu.make_async_copy(source, out.at[pl.ds(n * half, half)], sems.at[n, i])
+
+    def sides(piece):
+        return [
+            piece.at[pl.ds(pl.multiple_of(side * half, half), half)] for side in (core, 1 - core)
+        ]
+
+    def start(n, sources):
+        for copy in copies(n, sources):
+            copy.start()
+
     for n, k in ((0, jnp.where(core == 0, 0, 1)), (1, 2)):
         shift = x * 4 + (y - k // 2 + 4) % 4
         for s in range(NQ):
-
-            @pl.when(shift == s)
-            def _(n=n, s=s):
-                pltpu.make_async_copy(pieces[s], held.at[n], sems.at[n]).start()
+            if s == SPLIT:
+                two = [pieces[s], other]
+                pl.when((shift == s) & (core == 0))(functools.partial(start, n, two))
+                pl.when((shift == s) & (core == 1))(functools.partial(start, n, two[::-1]))
+            else:
+                piece = direct if (n, s) == (1, NQ - 1) else pieces[s]
+                pl.when(shift == s)(functools.partial(start, n, sides(piece)))
 
     for n in range(2):
-        pltpu.make_async_copy(pieces[0], held.at[n], sems.at[n]).wait()
-    for n in range(2):
-        at = slice(n * half, (n + 1) * half)
-        keep[at] = held[n, pl.ds(pl.multiple_of(core * half, half), half)]
-        give[at] = held[n, pl.ds(pl.multiple_of((1 - core) * half, half), half)]
+        for copy in copies(n, sides(pieces[0])):
+            copy.wait()
 
 
 def sort(pos, pieces):
@@ -247,39 +306,69 @@
     return pl.pallas_call(
         sort_kernel,
         out_shape=[shape, shape],
-        in_specs=[SM] + [ANY] * NQ,
+        in_specs=[SM] + [ANY] * (NQ + 2),
         out_specs=[VM, VM],
-        scratch_shapes=[
-            pltpu.VMEM((2, 2 * CH * B, B), F32),
-            pltpu.SemaphoreType.DMA((2,)),
-        ],
-        compiler_params=params(),
+        scratch_shapes=[pltpu.SemaphoreType.DMA((2, 2))],
+        compiler_params=params(4),
         cost_estimate=cost(2),
         name="sort",
     )(pos, *pieces)
 
 
-def panels_kernel(pos, inv, facing, keep, got, out):
-    first = pos[1] % 2 == 0
+def panels_kernel(pos, inv, facing, keep, got, out, held, chunk, load, store):
+    core = pos[1] % 2
     half = CH * B
-    w0 = jnp.where(first, keep[:half], got[:half])
-    w1 = jnp.where(first, got[:half], keep[:half])
-    w2 = jnp.where(first, keep[half:], got[half:])
-    n0 = dot_t(w0, inv[0], HI).astype(BF16)
-    out[:, :B] = n0
-    n1 = dot_t(w1 - dot_t(n0, facing[0]), inv[1], HI).astype(BF16)
-    out[:, B : 2 * B] = n1
-    rest = w2 - dot_t(n0, facing[1]) - dot_t(n1, facing[2])
-    out[:, 2 * B :] = dot_t(rest, inv[2], HI).astype(BF16)
+    lower, upper = pl.ds(0, half), pl.ds(half, half)
+
+    def copies(sources):
+        for k, (ref, at) in enumerate(sources):
+            yield pltpu.make_async_copy(ref.at[at], held.at[k], load.at[k])
+
+    even = ((keep, lower), (got, lower), (keep, upper))
+    odd = ((got, lower), (keep, lower), (got, upper))
+
+    @pl.when(core == 0)
+    def _():
+        for copy in copies(even):
+            copy.start()
+
+    @pl.when(core == 1)
+    def _():
+        for copy in copies(odd):
+            copy.start()
+
+    waits = list(copies(even))
+    waits[0].wait()
+    n0 = dot_t(held[0], inv[0], HI).astype(BF16)
+    chunk[:, :B] = n0
+    waits[1].wait()
+    n1 = dot_t(held[1] - dot_t(n0, facing[0]), inv[1], HI).astype(BF16)
+    chunk[:, B : 2 * B] = n1
+    waits[2].wait()
+    rest = held[2] - dot_t(n0, facing[1]) - dot_t(n1, facing[2])
+    chunk[:, 2 * B :] = dot_t(rest, inv[2], HI).astype(BF16)
+    stores = [
+        pltpu.make_async_copy(chunk, out.at[pl.ds(q * half, half)], store.at[q]) for q in range(NQ)
+    ]
+    for copy in stores:
+        copy.start()
+    for copy in stores:
+        copy.wait()
 
 
 def panels(pos, inv, facing, keep, got):
     return pl.pallas_call(
         panels_kernel,
-        out_shape=jax.ShapeDtypeStruct((CH * B, STEPS * B), BF16),
-        in_specs=[SM] + [VM] * 4,
-        out_specs=VM,
-        compiler_params=params(),
+        out_shape=jax.ShapeDtypeStruct((NQ * CH * B, STEPS * B), BF16),
+        in_specs=[SM, VM, VM, ANY, ANY],
+        out_specs=ANY,
+        scratch_shapes=[
+            pltpu.VMEM((STEPS, CH * B, B), F32),
+            pltpu.VMEM((CH * B, STEPS * B), BF16),
+            pltpu.SemaphoreType.DMA((STEPS,)),
+            pltpu.SemaphoreType.DMA((NQ,)),
+        ],
+        compiler_params=params(6),
         cost_estimate=cost(4),
         name="panels",
     )(pos, inv, facing, keep, got)
@@ -311,7 +400,7 @@
         out_shape=jax.ShapeDtypeStruct((ROWS, B), F32),
         in_specs=[SM, VM, VM, ANY],
         out_specs=VM,
-        compiler_params=params(),
+        compiler_params=params(12),
         cost_estimate=cost(20),
         name="solve",
     )(pos, work, inv, chunk)
@@ -340,14 +429,21 @@
         out_shape=jax.ShapeDtypeStruct((3, B, STEPS * B), BF16),
         in_specs=[SM, VM, VM],
         out_specs=VM,
-        compiler_params=params(),
+        compiler_params=params(3),
         cost_estimate=cost(1),
         name="across",
     )(pos, face, inv)
 
 
-def update_kernel(flip, pos, work, panel, parts, low, out, held, ins, outs):
+def update_kernel(flip, pos, work, narrow, parts, low, out, held, panel, ins, outs, reads):
     row, col = pos[0], pos[1]
+    size = CH * B
+    loads = [
+        pltpu.make_async_copy(
+            narrow.at[pl.ds(q * size, size)], panel.at[pl.ds(q * size, size)], reads.at[q]
+        )
+        for q in range(NQ)
+    ]
     core = (col + flip) % 2
 
     def each(q, there, act):
@@ -367,10 +463,12 @@
                 act(copy)
 
     for q in range(NQ):
+        loads[q].start()
         each(q, False, lambda copy: copy.start())
     for q in range(NQ):
         owner = 2 * q + core
-        rows = slice(q * CH * B, (q + 1) * CH * B)
+        rows = slice(q * size, (q + 1) * size)
+        loads[q].wait()
         each(q, False, lambda copy: copy.wait())
 
         @pl.when(col >= STEPS)
@@ -404,15 +502,17 @@
     return pl.pallas_call(
         functools.partial(update_kernel, flip),
         out_shape=jax.ShapeDtypeStruct((ROWS, B), F32),
-        in_specs=[SM, ANY, VM, VM, VM],
+        in_specs=[SM, ANY, ANY, VM, VM],
         out_specs=ANY,
         input_output_aliases={1: 0},
         scratch_shapes=[
             pltpu.VMEM((NQ, CH * B, B), F32),
+            pltpu.VMEM((NQ * CH * B, STEPS * B), BF16),
             pltpu.SemaphoreType.DMA((NQ, 2)),
             pltpu.SemaphoreType.DMA((NQ, 2)),
+            pltpu.SemaphoreType.DMA((NQ,)),
         ],
-        compiler_params=params(),
+        compiler_params=params(8),
         cost_estimate=cost(6),
         name="update",
     )(pos, work, panel, parts, low)
@@ -423,23 +523,29 @@
 
 
 def spread_top(front, row, col):
-    parts = [front[k * B : STEPS * B] for k in range(STEPS)]
-    second = send(parts[1], [((0, 1), (0, 0))])
-    third = send(parts[2], [((0, 2), (0, 0))])
-    root = (row == 0) & (col == 0)
-    top = jnp.where(root, jnp.concatenate([parts[0], second, third]), 0.0)
+    part = front[: STEPS * B]
+    a = send(part, [((0, 0), (0, 2)), ((0, 1), (0, 0)), ((0, 2), (0, 4))])
+    b = send(part, [((0, 0), (0, 4)), ((0, 1), (0, 2)), ((0, 2), (0, 6))])
+    c = send(part, [((0, 0), (0, 6)), ((0, 1), (0, 4)), ((0, 2), (0, 0))])
+    d = send(part, [((0, 1), (0, 6))])
+
+    def pick(at0, at2, at4, at6):
+        return jnp.where(col == 0, at0, jnp.where(col == 2, at2, jnp.where(col == 4, at4, at6)))
+
+    columns = [pick(part, a, b, c), pick(a, b, c, d), pick(c, part, a, b)]
+    rooted = (row == 0) & (col < NC // 2) & (col % 2 == 0)
+    top = jnp.concatenate([v[k * B :] for k, v in enumerate(columns)])
+    top = jnp.where(rooted, top, 0.0)
 
     def hop(top, *moves):
         return sum([send(top, pairs) for pairs in moves], top)
 
+    near = (0, 2, 4, 6)
+    beside = [[((0, c), (dr, c + dc)) for c in near] for dr, dc in ((0, 8), (1, 0), (1, 8))]
+    top = hop(top, *beside)
     even = range(0, NC, 2)
-    targets = (2, 6, 8, 4)
-    top = hop(top, *[[((0, 0), (0, c))] for c in targets])
-    top = hop(top, [((0, c), (0, c + 8)) for c in (2, 4, 6)])
-    top = hop(top, [((0, c), (1, c)) for c in even])
-    pair = [(r, c) for r in range(2) for c in even]
-    top = hop(top, [((r, c), (r + 2, c)) for r, c in pair], [((r, c), (r + 6, c)) for r, c in pair])
-    top = hop(top, [((r + 2, c), (r + 4, c)) for r, c in pair])
+    away = [[((r, c), (r + dr, c)) for r in range(2) for c in even] for dr in (4, 2, 6)]
+    top = hop(top, *away)
     return hop(top, [((r, c), (r, c + 1)) for c in even for r in range(NR)])
 
 
@@ -452,27 +558,26 @@
     low, inv, facing = factor(top)
     work, *chunks = assemble(pos, child_rows, front, got)
 
-    def outward(s):
-        pairs = []
-        for k in range(STEPS):
-            pairs.append((k, s // 4 * 8 + (k // 2 + s) % 4 * 2 + k % 2))
-        return lax.ppermute(chunks[s], "col", pairs)
-
     def home(k, dx, dy):
         return dx * 8 + (k // 2 + dy) % 4 * 2 + k % 2
 
+    def step(v, start, end, ks=range(STEPS)):
+        return lax.ppermute(v, "col", [(home(k, *start), home(k, *end)) for k in ks])
+
     pieces = {0: chunks[0]}
-    relayed = lax.ppermute(chunks[7], "col", [(k, home(k, 0, 3)) for k in range(STEPS)])
-    order = (1, 4, 2, 5, 3, 6)
-    for s in order:
-        pieces[s] = outward(s)
-    pieces[7] = lax.ppermute(relayed, "col", [(home(k, 0, 3), home(k, 1, 3)) for k in range(STEPS)])
-    keep, give = sort(pos, [pieces[s] for s in range(NQ)])
+    pairs = [(k, home(k, 0, 3)) for k in range(2)] + [(2, home(2, 1, 3))]
+    relayed = lax.ppermute(chunks[7], "col", pairs)
+    other = step(chunks[NQ], (0, 0), (0, 1))
+    for s in (4, 1, 5, 3, 6, 2):
+        pieces[s] = step(chunks[s], (0, 0), (s // 4, s % 4))
+    pieces[7] = step(relayed, (0, 3), (1, 3), range(2))
+    other = step(other, (0, 1), (1, 1))
+    keep, give = sort(pos, [pieces[s] for s in range(NQ)] + [other, relayed])
     flip = [(c, c ^ 1) for c in range(NC)]
     chunk = panels(pos, inv, facing, keep, lax.ppermute(give, "col", flip))
     cores = [[c for c in range(NC) if c % 2 == p] for p in range(2)]
     mine = lax.all_to_all(
-        jnp.tile(chunk, (NQ, 1)), "col", 0, 0, axis_index_groups=cores, tiled=True
+        chunk, "col", 0, 0, axis_index_groups=cores, tiled=True
     )
     face = jnp.where(row == 0, chunk[:B], jnp.zeros_like(chunk[:B]))
 

time: 220 us -> 194 us (0.88)
  blocking collectives: 58.5 us -> 47.8 us
  Pallas kernels: 58.9 us -> 50.3 us
  local copies, waits for them, and re-layouts: 8.77 us -> 2.3 us
  starting transfers between devices: 40 us -> 45.1 us
  waiting for transfers between devices: 48.4 us -> 43.4 us
    all_to_all x1, blocking collectives: 58.5 us -> 47.8 us  [on_device(): lax.all_to_all(chunk, 'col', 0, 0, axis_index_groups=cores, tiled=True)]
    ppermute x8 -> x10, starting transfers between devices: 19 us -> 25.7 us  [the longest x9 24.4 us: step(): lax.ppermute(v, 'col', [(home(k, *start), home(k, *end)) for k in ks])]
    all_to_all x1, waiting for transfers between devices: 18.5 us -> 13.9 us  [on_device(): got = lax.all_to_all(packed, 'row', 0, 0, tiled=True)]
    ppermute x4, waiting for transfers between devices: 8.34 us -> 12.5 us  [hop(): return sum([lax.ppermute(face, 'row', pairs) for pairs in moves], face)]
    unnamed x24 -> x8, local copies, waits for them, and re-layouts: 4.81 us -> 1.36 us
    ppermute x12 -> x11, waiting for transfers between devices: 7.3 us -> 5.02 us  [send(): lax.ppermute(x, ('row', 'col'), [(a * NC + b, c * NC + d) for (a, b), (c,...]
    ppermute x8 -> x10, waiting for transfers between devices: 14.3 us -> 12 us  [the longest x9 12 us: step(): lax.ppermute(v, 'col', [(home(k, *start), home(k, *end)) for k in ks])]
    ppermute x12 -> x11, starting transfers between devices: 10.9 us -> 9.44 us  [send(): lax.ppermute(x, ('row', 'col'), [(a * NC + b, c * NC + d) for (a, b), (c,...]
  transfers between devices with their start and end apart: 27 -> 28, of which waited for: 6 -> 7; matrix products, arithmetic and copies ran while one was open for 2% -> 2% of each run, Pallas kernels for 21% -> 18%
where the time goes in v2:
time: 194 us; the launch traced here: 193 us
  Pallas kernels  50.3 us (26%)
  blocking collectives  47.8 us (25%)
  starting transfers between devices  45.1 us (23%)
  waiting for transfers between devices  43.4 us (22%)
  other arithmetic  3.09 us (2%)
  local copies, waits for them, and re-layouts  2.3 us (1%)
    all_to_all x1, blocking collectives, on_device(): lax.all_to_all(chunk, 'col', 0, 0, axis_index_groups=cores, tiled=True)  47.8 us
    ppermute x9, starting transfers between devices, step(): lax.ppermute(v, 'col', [(home(k, *start), home(k, *end)) for k in ks])  24.4 us
    all_to_all x1, waiting for transfers between devices, on_device(): got = lax.all_to_all(packed, 'row', 0, 0, tiled=True)  13.9 us
    pallas_call x1, Pallas kernels, factor(): pl.pallas_call(factor_kernel, out_shape=[jax.ShapeDtypeStruct((STEPS, B,...  13 us
    ppermute x4, waiting for transfers between devices, hop(): return sum([lax.ppermute(face, 'row', pairs) for pairs in moves], face)  12.5 us
    pallas_call x2, Pallas kernels, update(): pl.pallas_call(functools.partial(update_kernel, flip), out_shape=jax.Shap...  12.4 us
    ppermute x9, waiting for transfers between devices, step(): lax.ppermute(v, 'col', [(home(k, *start), home(k, *end)) for k in ks])  12 us
    ppermute x11, starting transfers between devices, send(): lax.ppermute(x, ('row', 'col'), [(a * NC + b, c * NC + d) for (a, b), (c,...  9.44 us
  transfers between devices with their start and end apart: 28, of which 7 were waited for; matrix products, arithmetic and copies ran while one was open for 2% of the time, Pallas kernels for 18%

profile of v2, /device:TPU:72, one launch (start us, length us, event | category | flops | bytes accessed | tf_op | source)
XLA Modules:
  0.0 192.6 jit_solution(6193568510685748747)
XLA Ops:
  0.0 0.6 pad_add_fusion.pos
  0.6 4.1 %pack.1 = bf16[8192,128]{1,0:T(8,128)(2,1)} custom-call(s32[2]{0:T(128)} %pad_add_fusion.pos, s32[4,244]{1,0:T(4,128)} %rows.3, bf16[7808,128]{1,0:T(8,128)(2,1)} %child.1), custom_call_target="tpu_custom_call" | custom-call | flops 2700000000 | bytes 9000000 | tf_op jit(solution)/shard_map/pack/pallas_call | solution.py:65
  4.8 5.9 %all-to-all-start = ((bf16[8,1024,128]{2,1,0:T(8,128)(2,1)}), bf16[8,1024,128]{2,1,0:T(8,128)(2,1)S(1)}, u32[]{:S(2)}, u32[]{:S(2)}) async-start(bf16[8,1024,128]{2,1,0:T(8,128)(2,1)} %bitcast.10), calls=%async_computation | async-start | bytes 4194304 | tf_op jit(solution)/shard_map/all_to_all | solution.py:556
  10.7 0.9 slice.12
  11.6 0.7 collective-permute-start.2
  12.3 0.7 collective-permute-start.1
  13.0 0.7 collective-permute-start
  13.7 0.7 collective-permute-start.3
  14.5 1.0 select_select_fusion
  15.5 0.7 collective-permute-start.6
  16.2 0.7 collective-permute-start.5
  16.9 0.7 collective-permute-start.4
  17.7 0.7 collective-permute-start.9
  18.4 1.4 collective-permute-start.8
  19.8 1.3 collective-permute-start.7
  21.1 13.9 %all-to-all-done = bf16[8,1024,128]{2,1,0:T(8,128)(2,1)S(1)} async-done(((bf16[8,1024,128]{2,1,0:T(8,128)(2,1)}), bf16[8,1024,128]{2,1,0:T(8,128)(2,1)S(1)}, u32[]{:S(2)}, u32[]{:S(2)}) %all-to-all-start) | async-done | bytes 2097184 | tf_op jit(solution)/shard_map/all_to_all | solution.py:556
  35.0 1.3 copy-done.3
  36.4 7.8 %assemble.1 = (f32[7808,128]{1,0:T(8,128)}, f32[1024,128]{1,0:T(8,128)}, f32[1024,128]{1,0:T(8,128)}, f32[1024,128]{1,0:T(8,128)}, f32[1024,128]{1,0:T(8,128)}, ...) custom-call(s32[2]{0:T(128)} %pad_add_fusion.pos, ...), custom_call_target="tpu_custom_call" | custom-call | flops 5400000000 | bytes 18000000 | tf_op jit(solution)/shard_map/assemble/pallas_call | solution.py:152
  44.1 2.3 %collective-permute-start.19 = (f32[512,128]{1,0:T(8,128)}, f32[512,128]{1,0:T(8,128)S(1)}, u32[]{:S(2)}, u32[]{:S(2)}) collective-permute-start(f32[512,128]{1,0:T(8,128)} %get-tuple-element.31), channel_id=1, source_target_pairs={{0,2},{1,3},{2,4},{16,18},{17,19},{18,20},{32,34},{33,35},{34,36},... | collective-permute-start | bytes 786440 | tf_op jit(solution)/shard_map/ppermute | solution.py:565
  46.5 1.9 collective-permute-start.11
  48.4 1.3 collective-permute-start.17
  49.8 5.0 %collective-permute-done.7 = f32[768,128]{1,0:T(8,128)} collective-permute-done((f32[768,128]{1,0:T(8,128)S(1)}, f32[768,128]{1,0:T(8,128)}, u32[]{:S(2)}, u32[]{:S(2)}) %collective-permute-start.7) | collective-permute-done | bytes 393248 | tf_op jit(solution)/shard_map/ppermute | solution.py:522
  54.8 1.2 add_add_fusion
  56.0 1.3 collective-permute-start.10
  57.3 6.9 %collective-permute-start.15 = (f32[512,128]{1,0:T(8,128)}, f32[512,128]{1,0:T(8,128)S(1)}, u32[]{:S(2)}, u32[]{:S(2)}) collective-permute-start(f32[512,128]{1,0:T(8,128)} %get-tuple-element.28), channel_id=1, source_target_pairs={{0,10},{1,11},{2,12},{16,26},{17,27},{18,28},{32,42},{33,43},{34,4... | collective-permute-start | bytes 786440 | tf_op jit(solution)/shard_map/ppermute | solution.py:565
  64.2 1.3 collective-permute-start.20
  65.5 1.3 collective-permute-start.12
  66.9 1.5 collective-permute-done.15.refs_5_
  68.4 3.7 %collective-permute-start.13 = (f32[1024,128]{1,0:T(8,128)}, f32[1024,128]{1,0:T(8,128)S(1)}, u32[]{:S(2)}, u32[]{:S(2)}) collective-permute-start(f32[1024,128]{1,0:T(8,128)} %get-tuple-element.26), channel_id=1, source_target_pairs={{0,6},{1,7},{2,0},{16,22},{17,23},{18,16},{32,38},{33,39},{34,32},... | collective-permute-start | bytes 1572872 | tf_op jit(solution)/shard_map/ppermute | solution.py:565
  72.1 4.9 %collective-permute-start.14 = (f32[1024,128]{1,0:T(8,128)}, f32[1024,128]{1,0:T(8,128)S(1)}, u32[]{:S(2)}, u32[]{:S(2)}) collective-permute-start(f32[1024,128]{1,0:T(8,128)} %get-tuple-element.27), channel_id=1, source_target_pairs={{0,8},{1,9},{2,10},{16,24},{17,25},{18,26},{32,40},{33,41},{34,42}... | collective-permute-start | bytes 1572872 | tf_op jit(solution)/shard_map/ppermute | solution.py:565
  77.0 1.3 collective-permute-start.16
  78.3 0.7 collective-permute-start.18
  79.1 0.4 collective-permute-done.13.refs_3_
  79.5 4.5 %collective-permute-done.14.refs_4_ = f32[1024,128]{1,0:T(8,128)S(1)} collective-permute-done((f32[1024,128]{1,0:T(8,128)}, f32[1024,128]{1,0:T(8,128)S(1)}, u32[]{:S(2)}, u32[]{:S(2)}) %collective-permute-start.14) | collective-permute-done | bytes 524320 | tf_op jit(solution)/shard_map/ppermute | solution.py:565
  84.0 5.6 %collective-permute-done.16.refs_6_ = f32[1024,128]{1,0:T(8,128)S(1)} collective-permute-done((f32[1024,128]{1,0:T(8,128)}, f32[1024,128]{1,0:T(8,128)S(1)}, u32[]{:S(2)}, u32[]{:S(2)}) %collective-permute-start.16) | collective-permute-done | bytes 524320 | tf_op jit(solution)/shard_map/ppermute | solution.py:565
  89.6 0.8 sort.1
  90.5 13.0 %factor.1 = (f32[3,128,128]{2,1,0:T(8,128)S(1)}, f32[3,128,128]{2,1,0:T(8,128)S(1)}, bf16[3,128,128]{2,1,0:T(8,128)(2,1)S(1)}) custom-call(f32[768,128]{1,0:T(8,128)S(1)} %add.44.top), custom_call_target="tpu_custom_call" | custom-call | flops 13500000256 | bytes 45000000 | tf_op jit(solution)/shard_map/factor/pallas_call | solution.py:253
  103.5 4.1 %panels.1.chunk = bf16[4096,384]{1,0:T(8,128)(2,1)S(1)} custom-call(s32[2]{0:T(128)S(1)} %copy-done, f32[3,128,128]{2,1,0:T(8,128)S(1)} %get-tuple-element.21.inv, bf16[3,128,128]{2,1,0:T(8,128)(2,1)S(1)} %get-tuple-element.22.facing, f32[1024,128]{1,0:T(8,128)S(1)} %get-tuple-element.32.keep, f32[1024,128]{1,0:T(8,128)S(1)} %collective-permute-done.21.got), custom_call_target="tpu_custom_call" | custom-call | flops 3600000000 | bytes 12000000 | tf_op jit(solution)/shard_map/panels/pallas_call | solution.py:360
  107.7 47.8 %all_to_all.22 = bf16[8,512,384]{2,1,0:T(8,128)(2,1)S(1)} all-to-all(bf16[8,512,384]{2,1,0:T(8,128)(2,1)S(1)} %bitcast.6), channel_id=1, replica_groups={{0,2,4,6,8,10,12,14},{1,3,5,7,9,11,13,15},{16,18,20,22,24,26,28,30},{17..., dimensions={0} | all-to-all | bytes 6291456 | tf_op jit(solution)/shard_map/all_to_all | solution.py:579
  155.5 0.7 collective-permute-start.23
  156.2 0.7 collective-permute-start.22
  156.9 1.3 collective-permute-start.24
  158.2 12.4 %collective-permute-done.24 = bf16[128,384]{1,0:T(8,128)(2,1)S(1)} collective-permute-done((bf16[128,384]{1,0:T(8,128)(2,1)S(1)}, bf16[128,384]{1,0:T(8,128)(2,1)S(1)}, u32[]{:S(2)}, u32[]{:S(2)}) %collective-permute-start.24) | collective-permute-done | bytes 98336 | tf_op jit(solution)/shard_map/ppermute | solution.py:585
  170.7 1.3 collective-permute-start.25
  172.0 7.1 %solve.1.work = f32[7808,128]{1,0:T(8,128)} custom-call(s32[2]{0:T(128)S(1)} %copy-done, f32[7808,128]{1,0:T(8,128)S(1)} %copy-done.2, f32[3,128,128]{2,1,0:T(8,128)S(1)} %get-tuple-element.21.inv, bf16[4096,384]{1,0:T(8,128)(2,1)S(1)} %panels.1.chunk), custom_call_target="tpu_custom_call" | custom-call | flops 17999998976 | bytes 60000000 | tf_op jit(solution)/shard_map/solve/pallas_call | solution.py:398
  179.1 0.9 across.1.parts
  180.0 6.3 %update.2.work = f32[7808,128]{1,0:T(8,128)} custom-call(s32[2]{0:T(128)S(1)} %copy-done, f32[7808,128]{1,0:T(8,128)} %solve.1.work, bf16[4096,384]{1,0:T(8,128)(2,1)S(1)} %bitcast.8, bf16[3,128,384]{2,1,0:T(8,128)(2,1)S(1)} %across.1.parts, f32[3,128,128]{2,1,0:T(8,128)S(1)} %get-tuple-element.34.low), custom_call_target="tpu_custom_call", output_to_operand_aliasing={{}: (1, {})} | custom-call | flops 5400000000 | bytes 18000000 | tf_op jit(solution)/shard_map/update/pallas_call | solution.py:502
  186.4 6.1 %update.3 = f32[7808,128]{1,0:T(8,128)} custom-call(s32[2]{0:T(128)S(1)} %copy-done, f32[7808,128]{1,0:T(8,128)} %update.2.work, bf16[4096,384]{1,0:T(8,128)(2,1)S(1)} %collective-permute-done.26.narrow, bf16[3,128,384]{2,1,0:T(8,128)(2,1)S(1)} %across.1.parts, f32[3,128,128]{2,1,0:T(8,128)S(1)} %get-tuple-element.34.low), custom_call_target="tpu_custom_call", output_to_operand_aliasing={{}: (1, {})} | custom-call | flops 5400000000 | bytes 18000000 | tf_op jit(solution)/shard_map/update/pallas_call | solution.py:502
  (39 shorter events, 0.5 us)
Async XLA Ops:
  4.8 30.2 %all-to-all-start = ((bf16[8,1024,128]{2,1,0:T(8,128)(2,1)}), bf16[8,1024,128]{2,1,0:T(8,128)(2,1)S(1)}, u32[]{:S(2)}, u32[]{:S(2)}) async-start(bf16[8,1024,128]{2,1,0:T(8,128)(2,1)} %bitcast.10), calls=%async_computation | async-start | bytes 4194304 | tf_op jit(solution)/shard_map/all_to_all | solution.py:556
  11.6 2.8 %collective-permute-start.2 = (f32[384,128]{1,0:T(8,128)S(1)}, f32[384,128]{1,0:T(8,128)S(1)}, u32[]{:S(2)}, u32[]{:S(2)}) collective-permute-start(f32[384,128]{1,0:T(8,128)S(1)} %slice.12), channel_id=1, source_target_pairs={{0,6},{1,4},{2,0}} | collective-permute-start | bytes 589832 | tf_op jit(solution)/shard_map/ppermute | solution.py:522
  12.3 2.1 %collective-permute-start.1 = (f32[384,128]{1,0:T(8,128)S(1)}, f32[384,128]{1,0:T(8,128)S(1)}, u32[]{:S(2)}, u32[]{:S(2)}) collective-permute-start(f32[384,128]{1,0:T(8,128)S(1)} %slice.12), channel_id=1, source_target_pairs={{0,4},{1,2},{2,6}} | collective-permute-start | bytes 589832 | tf_op jit(solution)/shard_map/ppermute | solution.py:522
  13.0 1.4 collective-permute-start
  13.7 0.8 collective-permute-start.3
  15.5 2.1 %collective-permute-start.6 = (f32[768,128]{1,0:T(8,128)S(1)}, f32[768,128]{1,0:T(8,128)S(1)}, u32[]{:S(2)}, u32[]{:S(2)}) collective-permute-start(f32[768,128]{1,0:T(8,128)S(1)} %maximum_select_fusion), channel_id=1, source_target_pairs={{0,24},{2,26},{4,28},{6,30}} | collective-permute-start | bytes 1179656 | tf_op jit(solution)/shard_map/ppermute | solution.py:522
  16.2 1.4 collective-permute-start.5
  16.9 0.7 collective-permute-start.4
  17.7 30.7 %collective-permute-start.9 = (f32[768,128]{1,0:T(8,128)S(1)}, f32[768,128]{1,0:T(8,128)S(1)}, u32[]{:S(2)}, u32[]{:S(2)}) collective-permute-start(f32[768,128]{1,0:T(8,128)S(1)} %add_add_fusion.1), channel_id=1, source_target_pairs={{0,96},{2,98},{4,100},{6,102},{8,104},{10,106},{12,108},{14,110},{... | collective-permute-start | bytes 1179656 | tf_op jit(solution)/shard_map/ppermute | solution.py:522
  18.4 31.4 %collective-permute-start.8 = (f32[768,128]{1,0:T(8,128)S(1)}, f32[768,128]{1,0:T(8,128)}, u32[]{:S(2)}, u32[]{:S(2)}) collective-permute-start(f32[768,128]{1,0:T(8,128)S(1)} %add_add_fusion.1), channel_id=1, source_target_pairs={{0,32},{2,34},{4,36},{6,38},{8,40},{10,42},{12,44},{14,46},{16,48}... | collective-permute-start | bytes 1179656 | tf_op jit(solution)/shard_map/ppermute | solution.py:522
  19.8 34.9 %collective-permute-start.7 = (f32[768,128]{1,0:T(8,128)S(1)}, f32[768,128]{1,0:T(8,128)}, u32[]{:S(2)}, u32[]{:S(2)}) collective-permute-start(f32[768,128]{1,0:T(8,128)S(1)} %add_add_fusion.1), channel_id=1, source_target_pairs={{0,64},{2,66},{4,68},{6,70},{8,72},{10,74},{12,76},{14,78},{16,80}... | collective-permute-start | bytes 1179656 | tf_op jit(solution)/shard_map/ppermute | solution.py:522
  35.0 1.3 copy-start.3
  44.1 45.5 %copy-start = (s32[2]{0:T(128)S(1)}, s32[2]{0:T(128)}, u32[]{:S(2)}) copy-start(s32[2]{0:T(128)} %pad_add_fusion.pos) | copy-start | bytes 28
  44.1 45.5 %copy-start.1 = (f32[1024,128]{1,0:T(8,128)S(1)}, f32[1024,128]{1,0:T(8,128)}, u32[]{:S(2)}) copy-start(f32[1024,128]{1,0:T(8,128)} %get-tuple-element.23.refs_0_) | copy-start | bytes 1572868
  44.1 20.1 %collective-permute-start.19 = (f32[512,128]{1,0:T(8,128)}, f32[512,128]{1,0:T(8,128)S(1)}, u32[]{:S(2)}, u32[]{:S(2)}) collective-permute-start(f32[512,128]{1,0:T(8,128)} %get-tuple-element.31), channel_id=1, source_target_pairs={{0,2},{1,3},{2,4},{16,18},{17,19},{18,20},{32,34},{33,35},{34,36},... | collective-permute-start | bytes 786440 | tf_op jit(solution)/shard_map/ppermute | solution.py:565
  46.5 30.5 %collective-permute-start.11 = (f32[1024,128]{1,0:T(8,128)}, f32[1024,128]{1,0:T(8,128)S(1)}, u32[]{:S(2)}, u32[]{:S(2)}) collective-permute-start(f32[1024,128]{1,0:T(8,128)} %get-tuple-element.24), channel_id=1, source_target_pairs={{0,2},{1,3},{2,4},{16,18},{17,19},{18,20},{32,34},{33,35},{34,36},... | collective-permute-start | bytes 1572872 | tf_op jit(solution)/shard_map/ppermute | solution.py:565
  48.4 29.9 %collective-permute-start.17 = (f32[1024,128]{1,0:T(8,128)}, f32[1024,128]{1,0:T(8,128)S(1)}, u32[]{:S(2)}, u32[]{:S(2)}) collective-permute-start(f32[1024,128]{1,0:T(8,128)} %get-tuple-element.30), channel_id=1, source_target_pairs={{0,6},{1,7},{2,8},{16,22},{17,23},{18,24},{32,38},{33,39},{34,40},... | collective-permute-start | bytes 1572872 | tf_op jit(solution)/shard_map/ppermute | solution.py:569
  56.0 9.6 %collective-permute-start.10 = (f32[768,128]{1,0:T(8,128)S(1)}, f32[768,128]{1,0:T(8,128)S(1)}, u32[]{:S(2)}, u32[]{:S(2)}) collective-permute-start(f32[768,128]{1,0:T(8,128)S(1)} %add_add_fusion), channel_id=1, source_target_pairs={{0,1},{16,17},{32,33},{48,49},{64,65},{80,81},{96,97},{112,113},{2... | collective-permute-start | bytes 1179656 | tf_op jit(solution)/shard_map/ppermute | solution.py:522
  57.3 11.1 %collective-permute-start.15 = (f32[512,128]{1,0:T(8,128)}, f32[512,128]{1,0:T(8,128)S(1)}, u32[]{:S(2)}, u32[]{:S(2)}) collective-permute-start(f32[512,128]{1,0:T(8,128)} %get-tuple-element.28), channel_id=1, source_target_pairs={{0,10},{1,11},{2,12},{16,26},{17,27},{18,28},{32,42},{33,43},{34,4... | collective-permute-start | bytes 786440 | tf_op jit(solution)/shard_map/ppermute | solution.py:565
  64.2 7.8 %collective-permute-start.20 = (f32[512,128]{1,0:T(8,128)S(1)}, f32[512,128]{1,0:T(8,128)S(1)}, u32[]{:S(2)}, u32[]{:S(2)}) collective-permute-start(f32[512,128]{1,0:T(8,128)S(1)} %collective-permute-done.19), channel_id=1, source_target_pairs={{2,10},{3,11},{4,12},{18,26},{19,27},{20,28},{34,42},{35,43},{36,4... | collective-permute-start | bytes 786440 | tf_op jit(solution)/shard_map/ppermute | solution.py:565
  65.5 13.6 %collective-permute-start.12 = (f32[1024,128]{1,0:T(8,128)}, f32[1024,128]{1,0:T(8,128)S(1)}, u32[]{:S(2)}, u32[]{:S(2)}) collective-permute-start(f32[1024,128]{1,0:T(8,128)} %get-tuple-element.25), channel_id=1, source_target_pairs={{0,4},{1,5},{2,6},{16,20},{17,21},{18,22},{32,36},{33,37},{34,38},... | collective-permute-start | bytes 1572872 | tf_op jit(solution)/shard_map/ppermute | solution.py:565
  68.4 11.1 %collective-permute-start.13 = (f32[1024,128]{1,0:T(8,128)}, f32[1024,128]{1,0:T(8,128)S(1)}, u32[]{:S(2)}, u32[]{:S(2)}) collective-permute-start(f32[1024,128]{1,0:T(8,128)} %get-tuple-element.26), channel_id=1, source_target_pairs={{0,6},{1,7},{2,0},{16,22},{17,23},{18,16},{32,38},{33,39},{34,32},... | collective-permute-start | bytes 1572872 | tf_op jit(solution)/shard_map/ppermute | solution.py:565
  72.1 11.9 %collective-permute-start.14 = (f32[1024,128]{1,0:T(8,128)}, f32[1024,128]{1,0:T(8,128)S(1)}, u32[]{:S(2)}, u32[]{:S(2)}) collective-permute-start(f32[1024,128]{1,0:T(8,128)} %get-tuple-element.27), channel_id=1, source_target_pairs={{0,8},{1,9},{2,10},{16,24},{17,25},{18,26},{32,40},{33,41},{34,42}... | collective-permute-start | bytes 1572872 | tf_op jit(solution)/shard_map/ppermute | solution.py:565
  77.0 12.6 %collective-permute-start.16 = (f32[1024,128]{1,0:T(8,128)}, f32[1024,128]{1,0:T(8,128)S(1)}, u32[]{:S(2)}, u32[]{:S(2)}) collective-permute-start(f32[1024,128]{1,0:T(8,128)} %get-tuple-element.29), channel_id=1, source_target_pairs={{0,12},{1,13},{2,14},{16,28},{17,29},{18,30},{32,44},{33,45},{34,4... | collective-permute-start | bytes 1572872 | tf_op jit(solution)/shard_map/ppermute | solution.py:565
  78.3 11.2 %collective-permute-start.18 = (f32[1024,128]{1,0:T(8,128)S(1)}, f32[1024,128]{1,0:T(8,128)S(1)}, u32[]{:S(2)}, u32[]{:S(2)}) collective-permute-start(f32[1024,128]{1,0:T(8,128)S(1)} %collective-permute-done.17.refs_9_), channel_id=1, source_target_pairs={{6,14},{7,15},{22,30},{23,31},{38,46},{39,47},{54,62},{55,63},{70,... | collective-permute-start | bytes 1572872 | tf_op jit(solution)/shard_map/ppermute | solution.py:565
  90.4 13.1 %collective-permute-start.21 = (f32[1024,128]{1,0:T(8,128)S(1)}, f32[1024,128]{1,0:T(8,128)S(1)}, u32[]{:S(2)}, u32[]{:S(2)}) collective-permute-start(f32[1024,128]{1,0:T(8,128)S(1)} %get-tuple-element.33), channel_id=1, source_target_pairs={{0,1},{1,0},{2,3},{3,2},{4,5},{5,4},{6,7},{7,6},{8,9},{9,8},{10,11... | collective-permute-start | bytes 1572872 | tf_op jit(solution)/shard_map/ppermute | solution.py:577
  107.7 64.3 %copy-start.2 = (f32[7808,128]{1,0:T(8,128)S(1)}, f32[7808,128]{1,0:T(8,128)}, u32[]{:S(2)}) copy-start(f32[7808,128]{1,0:T(8,128)} %get-tuple-element.20.work) | copy-start | bytes 11993092
  155.5 30.9 %collective-permute-start.26 = (bf16[4096,384]{1,0:T(8,128)(2,1)S(1)}, bf16[4096,384]{1,0:T(8,128)(2,1)S(1)}, u32[]{:S(2)}, u32[]{:S(2)}) collective-permute-start(bf16[4096,384]{1,0:T(8,128)(2,1)S(1)} %bitcast.7), channel_id=1, source_target_pairs={{0,1},{1,0},{2,3},{3,2},{4,5},{5,4},{6,7},{7,6},{8,9},{9,8},{10,11... | collective-permute-start | bytes 9437192 | tf_op jit(solution)/shard_map/ppermute | solution.py:593
  155.5 1.4 collective-permute-start.23
  156.2 0.7 collective-permute-start.22
  156.9 13.7 %collective-permute-start.24 = (bf16[128,384]{1,0:T(8,128)(2,1)S(1)}, bf16[128,384]{1,0:T(8,128)(2,1)S(1)}, u32[]{:S(2)}, u32[]{:S(2)}) collective-permute-start(bf16[128,384]{1,0:T(8,128)(2,1)S(1)} %add_add_fusion.2), channel_id=1, source_target_pairs={{32,64},{33,65},{34,66},{35,67},{36,68},{37,69},{38,70},{39,71},{4... | collective-permute-start | bytes 294920 | tf_op jit(solution)/shard_map/ppermute | solution.py:585
  170.7 8.4 %collective-permute-start.25 = (bf16[128,384]{1,0:T(8,128)(2,1)S(1)}, bf16[128,384]{1,0:T(8,128)(2,1)S(1)}, u32[]{:S(2)}, u32[]{:S(2)}) collective-permute-start(bf16[128,384]{1,0:T(8,128)(2,1)S(1)} %add.47), channel_id=1, source_target_pairs={{0,16},{32,48},{64,80},{96,112},{1,17},{33,49},{65,81},{97,113},{2... | collective-permute-start | bytes 294920 | tf_op jit(solution)/shard_map/ppermute | solution.py:585

commit v3 on v2

--- a/solution.py
+++ b/solution.py
@@ -27,7 +27,7 @@
 
 
 def params(mib):
-    return pltpu.CompilerParams(vmem_limit_bytes=mib * 1024 * 1024)
+    return pltpu.CompilerParams(vmem_limit_bytes=int(mib * 1024 * 1024))
 
 
 def cost(us):
@@ -169,8 +169,8 @@
     )(pos, rows, front, got)
 
 
-NB = 32
-NW = 8
+NB = 64
+NW = 16
 
 
 def eliminate(m):
@@ -435,15 +435,9 @@
     )(pos, face, inv)
 
 
-def update_kernel(flip, pos, work, narrow, parts, low, out, held, panel, ins, outs, reads):
+def update_kernel(flip, pos, work, panel, parts, low, out, held, ins, outs):
     row, col = pos[0], pos[1]
     size = CH * B
-    loads = [
-        pltpu.make_async_copy(
-            narrow.at[pl.ds(q * size, size)], panel.at[pl.ds(q * size, size)], reads.at[q]
-        )
-        for q in range(NQ)
-    ]
     core = (col + flip) % 2
 
     def each(q, there, act):
@@ -463,12 +457,10 @@
                 act(copy)
 
     for q in range(NQ):
-        loads[q].start()
         each(q, False, lambda copy: copy.start())
     for q in range(NQ):
         owner = 2 * q + core
         rows = slice(q * size, (q + 1) * size)
-        loads[q].wait()
         each(q, False, lambda copy: copy.wait())
 
         @pl.when(col >= STEPS)
@@ -502,15 +494,13 @@
     return pl.pallas_call(
         functools.partial(update_kernel, flip),
         out_shape=jax.ShapeDtypeStruct((ROWS, B), F32),
-        in_specs=[SM, ANY, ANY, VM, VM],
+        in_specs=[SM, ANY, VM, VM, VM],
         out_specs=ANY,
         input_output_aliases={1: 0},
         scratch_shapes=[
             pltpu.VMEM((NQ, CH * B, B), F32),
-            pltpu.VMEM((NQ * CH * B, STEPS * B), BF16),
             pltpu.SemaphoreType.DMA((NQ, 2)),
             pltpu.SemaphoreType.DMA((NQ, 2)),
-            pltpu.SemaphoreType.DMA((NQ,)),
         ],
         compiler_params=params(8),
         cost_estimate=cost(6),

time: 194 us -> 191 us (0.985)
  Pallas kernels: 50.3 us -> 47.9 us
where the time goes in v3:
time: 191 us; the launch traced here: 190 us
  Pallas kernels  47.9 us (25%)
  blocking collectives  47.8 us (25%)
  starting transfers between devices  45.1 us (24%)
  waiting for transfers between devices  43.4 us (23%)
  other arithmetic  3.09 us (2%)
  local copies, waits for them, and re-layouts  2.3 us (1%)
    all_to_all x1, blocking collectives, on_device(): lax.all_to_all(chunk, 'col', 0, 0, axis_index_groups=cores, tiled=True)  47.8 us
    ppermute x9, starting transfers between devices, step(): lax.ppermute(v, 'col', [(home(k, *start), home(k, *end)) for k in ks])  24.4 us
    all_to_all x1, waiting for transfers between devices, on_device(): got = lax.all_to_all(packed, 'row', 0, 0, tiled=True)  13.9 us
    ppermute x4, waiting for transfers between devices, hop(): return sum([lax.ppermute(face, 'row', pairs) for pairs in moves], face)  12.5 us
    ppermute x9, waiting for transfers between devices, step(): lax.ppermute(v, 'col', [(home(k, *start), home(k, *end)) for k in ks])  12 us
    pallas_call x1, Pallas kernels, factor(): pl.pallas_call(factor_kernel, out_shape=[jax.ShapeDtypeStruct((STEPS, B,...  11.9 us
    pallas_call x2, Pallas kernels, update(): pl.pallas_call(functools.partial(update_kernel, flip), out_shape=jax.Shap...  11 us
    ppermute x11, starting transfers between devices, send(): lax.ppermute(x, ('row', 'col'), [(a * NC + b, c * NC + d) for (a, b), (c,...  9.44 us
  transfers between devices with their start and end apart: 28, of which 7 were waited for; matrix products, arithmetic and copies ran while one was open for 2% of the time, Pallas kernels for 18%

profile of v3, /device:TPU:72, one launch (start us, length us, event | category | flops | bytes accessed | tf_op | source)
XLA Modules:
  0.0 190.3 jit_solution(5927771517509615546)
XLA Ops:
  0.0 0.6 pad_add_fusion.pos
  0.6 4.1 %pack.1 = bf16[8192,128]{1,0:T(8,128)(2,1)} custom-call(s32[2]{0:T(128)} %pad_add_fusion.pos, s32[4,244]{1,0:T(4,128)} %rows.3, bf16[7808,128]{1,0:T(8,128)(2,1)} %child.1), custom_call_target="tpu_custom_call" | custom-call | flops 2700000000 | bytes 9000000 | tf_op jit(solution)/shard_map/pack/pallas_call | solution.py:65
  4.8 5.9 %all-to-all-start = ((bf16[8,1024,128]{2,1,0:T(8,128)(2,1)}), bf16[8,1024,128]{2,1,0:T(8,128)(2,1)S(1)}, u32[]{:S(2)}, u32[]{:S(2)}) async-start(bf16[8,1024,128]{2,1,0:T(8,128)(2,1)} %bitcast.10), calls=%async_computation | async-start | bytes 4194304 | tf_op jit(solution)/shard_map/all_to_all | solution.py:546
  10.7 0.9 slice.12
  11.6 0.7 collective-permute-start.2
  12.3 0.7 collective-permute-start.1
  13.0 0.7 collective-permute-start
  13.7 0.7 collective-permute-start.3
  14.5 1.0 select_select_fusion
  15.5 0.7 collective-permute-start.6
  16.2 0.7 collective-permute-start.5
  16.9 0.7 collective-permute-start.4
  17.7 0.7 collective-permute-start.9
  18.4 1.4 collective-permute-start.8
  19.8 1.3 collective-permute-start.7
  21.1 13.9 %all-to-all-done = bf16[8,1024,128]{2,1,0:T(8,128)(2,1)S(1)} async-done(((bf16[8,1024,128]{2,1,0:T(8,128)(2,1)}), bf16[8,1024,128]{2,1,0:T(8,128)(2,1)S(1)}, u32[]{:S(2)}, u32[]{:S(2)}) %all-to-all-start) | async-done | bytes 2097184 | tf_op jit(solution)/shard_map/all_to_all | solution.py:546
  35.0 1.3 copy-done.3
  36.4 7.8 %assemble.1 = (f32[7808,128]{1,0:T(8,128)}, f32[1024,128]{1,0:T(8,128)}, f32[1024,128]{1,0:T(8,128)}, f32[1024,128]{1,0:T(8,128)}, f32[1024,128]{1,0:T(8,128)}, ...) custom-call(s32[2]{0:T(128)} %pad_add_fusion.pos, ...), custom_call_target="tpu_custom_call" | custom-call | flops 5400000000 | bytes 18000000 | tf_op jit(solution)/shard_map/assemble/pallas_call | solution.py:152
  44.1 2.3 %collective-permute-start.19 = (f32[512,128]{1,0:T(8,128)}, f32[512,128]{1,0:T(8,128)S(1)}, u32[]{:S(2)}, u32[]{:S(2)}) collective-permute-start(f32[512,128]{1,0:T(8,128)} %get-tuple-element.31), channel_id=1, source_target_pairs={{0,2},{1,3},{2,4},{16,18},{17,19},{18,20},{32,34},{33,35},{34,36},... | collective-permute-start | bytes 786440 | tf_op jit(solution)/shard_map/ppermute | solution.py:555
  46.5 1.9 %collective-permute-start.11 = (f32[1024,128]{1,0:T(8,128)}, f32[1024,128]{1,0:T(8,128)S(1)}, u32[]{:S(2)}, u32[]{:S(2)}) collective-permute-start(f32[1024,128]{1,0:T(8,128)} %get-tuple-element.24), channel_id=1, source_target_pairs={{0,2},{1,3},{2,4},{16,18},{17,19},{18,20},{32,34},{33,35},{34,36},... | collective-permute-start | bytes 1572872 | tf_op jit(solution)/shard_map/ppermute | solution.py:555
  48.4 1.3 collective-permute-start.17
  49.8 5.0 %collective-permute-done.7 = f32[768,128]{1,0:T(8,128)} collective-permute-done((f32[768,128]{1,0:T(8,128)S(1)}, f32[768,128]{1,0:T(8,128)}, u32[]{:S(2)}, u32[]{:S(2)}) %collective-permute-start.7) | collective-permute-done | bytes 393248 | tf_op jit(solution)/shard_map/ppermute | solution.py:512
  54.8 1.2 add_add_fusion
  56.0 1.3 collective-permute-start.10
  57.3 6.9 %collective-permute-start.15 = (f32[512,128]{1,0:T(8,128)}, f32[512,128]{1,0:T(8,128)S(1)}, u32[]{:S(2)}, u32[]{:S(2)}) collective-permute-start(f32[512,128]{1,0:T(8,128)} %get-tuple-element.28), channel_id=1, source_target_pairs={{0,10},{1,11},{2,12},{16,26},{17,27},{18,28},{32,42},{33,43},{34,4... | collective-permute-start | bytes 786440 | tf_op jit(solution)/shard_map/ppermute | solution.py:555
  64.2 1.3 collective-permute-start.20
  65.5 1.3 collective-permute-start.12
  66.9 1.5 collective-permute-done.15.refs_5_
  68.4 3.7 %collective-permute-start.13 = (f32[1024,128]{1,0:T(8,128)}, f32[1024,128]{1,0:T(8,128)S(1)}, u32[]{:S(2)}, u32[]{:S(2)}) collective-permute-start(f32[1024,128]{1,0:T(8,128)} %get-tuple-element.26), channel_id=1, source_target_pairs={{0,6},{1,7},{2,0},{16,22},{17,23},{18,16},{32,38},{33,39},{34,32},... | collective-permute-start | bytes 1572872 | tf_op jit(solution)/shard_map/ppermute | solution.py:555
  72.1 4.9 %collective-permute-start.14 = (f32[1024,128]{1,0:T(8,128)}, f32[1024,128]{1,0:T(8,128)S(1)}, u32[]{:S(2)}, u32[]{:S(2)}) collective-permute-start(f32[1024,128]{1,0:T(8,128)} %get-tuple-element.27), channel_id=1, source_target_pairs={{0,8},{1,9},{2,10},{16,24},{17,25},{18,26},{32,40},{33,41},{34,42}... | collective-permute-start | bytes 1572872 | tf_op jit(solution)/shard_map/ppermute | solution.py:555
  77.0 1.3 collective-permute-start.16
  78.3 0.7 collective-permute-start.18
  79.1 0.4 collective-permute-done.13.refs_3_
  79.5 4.5 %collective-permute-done.14.refs_4_ = f32[1024,128]{1,0:T(8,128)S(1)} collective-permute-done((f32[1024,128]{1,0:T(8,128)}, f32[1024,128]{1,0:T(8,128)S(1)}, u32[]{:S(2)}, u32[]{:S(2)}) %collective-permute-start.14) | collective-permute-done | bytes 524320 | tf_op jit(solution)/shard_map/ppermute | solution.py:555
  84.0 5.6 %collective-permute-done.16.refs_6_ = f32[1024,128]{1,0:T(8,128)S(1)} collective-permute-done((f32[1024,128]{1,0:T(8,128)}, f32[1024,128]{1,0:T(8,128)S(1)}, u32[]{:S(2)}, u32[]{:S(2)}) %collective-permute-start.16) | collective-permute-done | bytes 524320 | tf_op jit(solution)/shard_map/ppermute | solution.py:555
  89.6 0.8 sort.1
  90.5 11.9 %factor.1 = (f32[3,128,128]{2,1,0:T(8,128)S(1)}, f32[3,128,128]{2,1,0:T(8,128)S(1)}, bf16[3,128,128]{2,1,0:T(8,128)(2,1)S(1)}) custom-call(f32[768,128]{1,0:T(8,128)S(1)} %add.44.top), custom_call_target="tpu_custom_call" | custom-call | flops 13500000256 | bytes 45000000 | tf_op jit(solution)/shard_map/factor/pallas_call | solution.py:253
  102.4 4.1 %panels.1.chunk = bf16[4096,384]{1,0:T(8,128)(2,1)S(1)} custom-call(s32[2]{0:T(128)S(1)} %copy-done, f32[3,128,128]{2,1,0:T(8,128)S(1)} %get-tuple-element.21.inv, bf16[3,128,128]{2,1,0:T(8,128)(2,1)S(1)} %get-tuple-element.22.facing, f32[1024,128]{1,0:T(8,128)S(1)} %get-tuple-element.32.keep, f32[1024,128]{1,0:T(8,128)S(1)} %collective-permute-done.21.got), custom_call_target="tpu_custom_call" | custom-call | flops 3600000000 | bytes 12000000 | tf_op jit(solution)/shard_map/panels/pallas_call | solution.py:360
  106.5 47.8 %all_to_all.22 = bf16[8,512,384]{2,1,0:T(8,128)(2,1)S(1)} all-to-all(bf16[8,512,384]{2,1,0:T(8,128)(2,1)S(1)} %bitcast.6), channel_id=1, replica_groups={{0,2,4,6,8,10,12,14},{1,3,5,7,9,11,13,15},{16,18,20,22,24,26,28,30},{17..., dimensions={0} | all-to-all | bytes 6291456 | tf_op jit(solution)/shard_map/all_to_all | solution.py:569
  154.4 0.7 collective-permute-start.23
  155.0 0.7 collective-permute-start.22
  155.8 1.3 collective-permute-start.24
  157.1 12.5 %collective-permute-done.24 = bf16[128,384]{1,0:T(8,128)(2,1)S(1)} collective-permute-done((bf16[128,384]{1,0:T(8,128)(2,1)S(1)}, bf16[128,384]{1,0:T(8,128)(2,1)S(1)}, u32[]{:S(2)}, u32[]{:S(2)}) %collective-permute-start.24) | collective-permute-done | bytes 98336 | tf_op jit(solution)/shard_map/ppermute | solution.py:575
  169.6 1.3 collective-permute-start.25
  170.9 7.3 %solve.1.work = f32[7808,128]{1,0:T(8,128)} custom-call(s32[2]{0:T(128)S(1)} %copy-done, f32[7808,128]{1,0:T(8,128)S(1)} %copy-done.2, f32[3,128,128]{2,1,0:T(8,128)S(1)} %get-tuple-element.21.inv, bf16[4096,384]{1,0:T(8,128)(2,1)S(1)} %panels.1.chunk), custom_call_target="tpu_custom_call" | custom-call | flops 17999998976 | bytes 60000000 | tf_op jit(solution)/shard_map/solve/pallas_call | solution.py:398
  178.2 0.9 across.1.parts
  179.1 5.5 %update.2.work = f32[7808,128]{1,0:T(8,128)} custom-call(s32[2]{0:T(128)S(1)} %copy-done, f32[7808,128]{1,0:T(8,128)} %solve.1.work, bf16[4096,384]{1,0:T(8,128)(2,1)S(1)} %bitcast.8, bf16[3,128,384]{2,1,0:T(8,128)(2,1)S(1)} %across.1.parts, f32[3,128,128]{2,1,0:T(8,128)S(1)} %get-tuple-element.34.low), custom_call_target="tpu_custom_call", output_to_operand_aliasing={{}: (1, {})} | custom-call | flops 5400000000 | bytes 18000000 | tf_op jit(solution)/shard_map/update/pallas_call | solution.py:494
  184.6 5.5 %update.3 = f32[7808,128]{1,0:T(8,128)} custom-call(s32[2]{0:T(128)S(1)} %copy-done, f32[7808,128]{1,0:T(8,128)} %update.2.work, bf16[4096,384]{1,0:T(8,128)(2,1)S(1)} %collective-permute-done.26.panel, bf16[3,128,384]{2,1,0:T(8,128)(2,1)S(1)} %across.1.parts, f32[3,128,128]{2,1,0:T(8,128)S(1)} %get-tuple-element.34.low), custom_call_target="tpu_custom_call", output_to_operand_aliasing={{}: (1, {})} | custom-call | flops 5400000000 | bytes 18000000 | tf_op jit(solution)/shard_map/update/pallas_call | solution.py:494
  (39 shorter events, 0.5 us)
Async XLA Ops:
  4.8 30.2 %all-to-all-start = ((bf16[8,1024,128]{2,1,0:T(8,128)(2,1)}), bf16[8,1024,128]{2,1,0:T(8,128)(2,1)S(1)}, u32[]{:S(2)}, u32[]{:S(2)}) async-start(bf16[8,1024,128]{2,1,0:T(8,128)(2,1)} %bitcast.10), calls=%async_computation | async-start | bytes 4194304 | tf_op jit(solution)/shard_map/all_to_all | solution.py:546
  11.6 2.8 %collective-permute-start.2 = (f32[384,128]{1,0:T(8,128)S(1)}, f32[384,128]{1,0:T(8,128)S(1)}, u32[]{:S(2)}, u32[]{:S(2)}) collective-permute-start(f32[384,128]{1,0:T(8,128)S(1)} %slice.12), channel_id=1, source_target_pairs={{0,6},{1,4},{2,0}} | collective-permute-start | bytes 589832 | tf_op jit(solution)/shard_map/ppermute | solution.py:512
  12.3 2.1 %collective-permute-start.1 = (f32[384,128]{1,0:T(8,128)S(1)}, f32[384,128]{1,0:T(8,128)S(1)}, u32[]{:S(2)}, u32[]{:S(2)}) collective-permute-start(f32[384,128]{1,0:T(8,128)S(1)} %slice.12), channel_id=1, source_target_pairs={{0,4},{1,2},{2,6}} | collective-permute-start | bytes 589832 | tf_op jit(solution)/shard_map/ppermute | solution.py:512
  13.0 1.4 collective-permute-start
  13.7 0.8 collective-permute-start.3
  15.5 2.1 %collective-permute-start.6 = (f32[768,128]{1,0:T(8,128)S(1)}, f32[768,128]{1,0:T(8,128)S(1)}, u32[]{:S(2)}, u32[]{:S(2)}) collective-permute-start(f32[768,128]{1,0:T(8,128)S(1)} %maximum_select_fusion), channel_id=1, source_target_pairs={{0,24},{2,26},{4,28},{6,30}} | collective-permute-start | bytes 1179656 | tf_op jit(solution)/shard_map/ppermute | solution.py:512
  16.2 1.4 collective-permute-start.5
  16.9 0.7 collective-permute-start.4
  17.7 30.7 %collective-permute-start.9 = (f32[768,128]{1,0:T(8,128)S(1)}, f32[768,128]{1,0:T(8,128)S(1)}, u32[]{:S(2)}, u32[]{:S(2)}) collective-permute-start(f32[768,128]{1,0:T(8,128)S(1)} %add_add_fusion.1), channel_id=1, source_target_pairs={{0,96},{2,98},{4,100},{6,102},{8,104},{10,106},{12,108},{14,110},{... | collective-permute-start | bytes 1179656 | tf_op jit(solution)/shard_map/ppermute | solution.py:512
  18.4 31.4 %collective-permute-start.8 = (f32[768,128]{1,0:T(8,128)S(1)}, f32[768,128]{1,0:T(8,128)}, u32[]{:S(2)}, u32[]{:S(2)}) collective-permute-start(f32[768,128]{1,0:T(8,128)S(1)} %add_add_fusion.1), channel_id=1, source_target_pairs={{0,32},{2,34},{4,36},{6,38},{8,40},{10,42},{12,44},{14,46},{16,48}... | collective-permute-start | bytes 1179656 | tf_op jit(solution)/shard_map/ppermute | solution.py:512
  19.8 34.9 %collective-permute-start.7 = (f32[768,128]{1,0:T(8,128)S(1)}, f32[768,128]{1,0:T(8,128)}, u32[]{:S(2)}, u32[]{:S(2)}) collective-permute-start(f32[768,128]{1,0:T(8,128)S(1)} %add_add_fusion.1), channel_id=1, source_target_pairs={{0,64},{2,66},{4,68},{6,70},{8,72},{10,74},{12,76},{14,78},{16,80}... | collective-permute-start | bytes 1179656 | tf_op jit(solution)/shard_map/ppermute | solution.py:512
  35.0 1.3 copy-start.3
  44.1 45.5 %copy-start = (s32[2]{0:T(128)S(1)}, s32[2]{0:T(128)}, u32[]{:S(2)}) copy-start(s32[2]{0:T(128)} %pad_add_fusion.pos) | copy-start | bytes 28
  44.1 45.5 %copy-start.1 = (f32[1024,128]{1,0:T(8,128)S(1)}, f32[1024,128]{1,0:T(8,128)}, u32[]{:S(2)}) copy-start(f32[1024,128]{1,0:T(8,128)} %get-tuple-element.23.refs_0_) | copy-start | bytes 1572868
  44.1 20.1 %collective-permute-start.19 = (f32[512,128]{1,0:T(8,128)}, f32[512,128]{1,0:T(8,128)S(1)}, u32[]{:S(2)}, u32[]{:S(2)}) collective-permute-start(f32[512,128]{1,0:T(8,128)} %get-tuple-element.31), channel_id=1, source_target_pairs={{0,2},{1,3},{2,4},{16,18},{17,19},{18,20},{32,34},{33,35},{34,36},... | collective-permute-start | bytes 786440 | tf_op jit(solution)/shard_map/ppermute | solution.py:555
  46.5 30.5 %collective-permute-start.11 = (f32[1024,128]{1,0:T(8,128)}, f32[1024,128]{1,0:T(8,128)S(1)}, u32[]{:S(2)}, u32[]{:S(2)}) collective-permute-start(f32[1024,128]{1,0:T(8,128)} %get-tuple-element.24), channel_id=1, source_target_pairs={{0,2},{1,3},{2,4},{16,18},{17,19},{18,20},{32,34},{33,35},{34,36},... | collective-permute-start | bytes 1572872 | tf_op jit(solution)/shard_map/ppermute | solution.py:555
  48.4 29.9 %collective-permute-start.17 = (f32[1024,128]{1,0:T(8,128)}, f32[1024,128]{1,0:T(8,128)S(1)}, u32[]{:S(2)}, u32[]{:S(2)}) collective-permute-start(f32[1024,128]{1,0:T(8,128)} %get-tuple-element.30), channel_id=1, source_target_pairs={{0,6},{1,7},{2,8},{16,22},{17,23},{18,24},{32,38},{33,39},{34,40},... | collective-permute-start | bytes 1572872 | tf_op jit(solution)/shard_map/ppermute | solution.py:559
  56.0 9.6 %collective-permute-start.10 = (f32[768,128]{1,0:T(8,128)S(1)}, f32[768,128]{1,0:T(8,128)S(1)}, u32[]{:S(2)}, u32[]{:S(2)}) collective-permute-start(f32[768,128]{1,0:T(8,128)S(1)} %add_add_fusion), channel_id=1, source_target_pairs={{0,1},{16,17},{32,33},{48,49},{64,65},{80,81},{96,97},{112,113},{2... | collective-permute-start | bytes 1179656 | tf_op jit(solution)/shard_map/ppermute | solution.py:512
  57.3 11.1 %collective-permute-start.15 = (f32[512,128]{1,0:T(8,128)}, f32[512,128]{1,0:T(8,128)S(1)}, u32[]{:S(2)}, u32[]{:S(2)}) collective-permute-start(f32[512,128]{1,0:T(8,128)} %get-tuple-element.28), channel_id=1, source_target_pairs={{0,10},{1,11},{2,12},{16,26},{17,27},{18,28},{32,42},{33,43},{34,4... | collective-permute-start | bytes 786440 | tf_op jit(solution)/shard_map/ppermute | solution.py:555
  64.2 7.8 %collective-permute-start.20 = (f32[512,128]{1,0:T(8,128)S(1)}, f32[512,128]{1,0:T(8,128)S(1)}, u32[]{:S(2)}, u32[]{:S(2)}) collective-permute-start(f32[512,128]{1,0:T(8,128)S(1)} %collective-permute-done.19), channel_id=1, source_target_pairs={{2,10},{3,11},{4,12},{18,26},{19,27},{20,28},{34,42},{35,43},{36,4... | collective-permute-start | bytes 786440 | tf_op jit(solution)/shard_map/ppermute | solution.py:555
  65.5 13.6 %collective-permute-start.12 = (f32[1024,128]{1,0:T(8,128)}, f32[1024,128]{1,0:T(8,128)S(1)}, u32[]{:S(2)}, u32[]{:S(2)}) collective-permute-start(f32[1024,128]{1,0:T(8,128)} %get-tuple-element.25), channel_id=1, source_target_pairs={{0,4},{1,5},{2,6},{16,20},{17,21},{18,22},{32,36},{33,37},{34,38},... | collective-permute-start | bytes 1572872 | tf_op jit(solution)/shard_map/ppermute | solution.py:555
  68.4 11.1 %collective-permute-start.13 = (f32[1024,128]{1,0:T(8,128)}, f32[1024,128]{1,0:T(8,128)S(1)}, u32[]{:S(2)}, u32[]{:S(2)}) collective-permute-start(f32[1024,128]{1,0:T(8,128)} %get-tuple-element.26), channel_id=1, source_target_pairs={{0,6},{1,7},{2,0},{16,22},{17,23},{18,16},{32,38},{33,39},{34,32},... | collective-permute-start | bytes 1572872 | tf_op jit(solution)/shard_map/ppermute | solution.py:555
  72.1 11.9 %collective-permute-start.14 = (f32[1024,128]{1,0:T(8,128)}, f32[1024,128]{1,0:T(8,128)S(1)}, u32[]{:S(2)}, u32[]{:S(2)}) collective-permute-start(f32[1024,128]{1,0:T(8,128)} %get-tuple-element.27), channel_id=1, source_target_pairs={{0,8},{1,9},{2,10},{16,24},{17,25},{18,26},{32,40},{33,41},{34,42}... | collective-permute-start | bytes 1572872 | tf_op jit(solution)/shard_map/ppermute | solution.py:555
  77.0 12.6 %collective-permute-start.16 = (f32[1024,128]{1,0:T(8,128)}, f32[1024,128]{1,0:T(8,128)S(1)}, u32[]{:S(2)}, u32[]{:S(2)}) collective-permute-start(f32[1024,128]{1,0:T(8,128)} %get-tuple-element.29), channel_id=1, source_target_pairs={{0,12},{1,13},{2,14},{16,28},{17,29},{18,30},{32,44},{33,45},{34,4... | collective-permute-start | bytes 1572872 | tf_op jit(solution)/shard_map/ppermute | solution.py:555
  78.3 11.2 %collective-permute-start.18 = (f32[1024,128]{1,0:T(8,128)S(1)}, f32[1024,128]{1,0:T(8,128)S(1)}, u32[]{:S(2)}, u32[]{:S(2)}) collective-permute-start(f32[1024,128]{1,0:T(8,128)S(1)} %collective-permute-done.17.refs_9_), channel_id=1, source_target_pairs={{6,14},{7,15},{22,30},{23,31},{38,46},{39,47},{54,62},{55,63},{70,... | collective-permute-start | bytes 1572872 | tf_op jit(solution)/shard_map/ppermute | solution.py:555
  90.4 12.0 %collective-permute-start.21 = (f32[1024,128]{1,0:T(8,128)S(1)}, f32[1024,128]{1,0:T(8,128)S(1)}, u32[]{:S(2)}, u32[]{:S(2)}) collective-permute-start(f32[1024,128]{1,0:T(8,128)S(1)} %get-tuple-element.33), channel_id=1, source_target_pairs={{0,1},{1,0},{2,3},{3,2},{4,5},{5,4},{6,7},{7,6},{8,9},{9,8},{10,11... | collective-permute-start | bytes 1572872 | tf_op jit(solution)/shard_map/ppermute | solution.py:567
  106.5 64.3 %copy-start.2 = (f32[7808,128]{1,0:T(8,128)S(1)}, f32[7808,128]{1,0:T(8,128)}, u32[]{:S(2)}) copy-start(f32[7808,128]{1,0:T(8,128)} %get-tuple-element.20.work) | copy-start | bytes 11993092
  154.3 30.3 %collective-permute-start.26 = (bf16[4096,384]{1,0:T(8,128)(2,1)S(1)}, bf16[4096,384]{1,0:T(8,128)(2,1)S(1)}, u32[]{:S(2)}, u32[]{:S(2)}) collective-permute-start(bf16[4096,384]{1,0:T(8,128)(2,1)S(1)} %bitcast.7), channel_id=1, source_target_pairs={{0,1},{1,0},{2,3},{3,2},{4,5},{5,4},{6,7},{7,6},{8,9},{9,8},{10,11... | collective-permute-start | bytes 9437192 | tf_op jit(solution)/shard_map/ppermute | solution.py:583
  154.4 1.4 collective-permute-start.23
  155.0 0.7 collective-permute-start.22
  155.8 13.8 %collective-permute-start.24 = (bf16[128,384]{1,0:T(8,128)(2,1)S(1)}, bf16[128,384]{1,0:T(8,128)(2,1)S(1)}, u32[]{:S(2)}, u32[]{:S(2)}) collective-permute-start(bf16[128,384]{1,0:T(8,128)(2,1)S(1)} %add_add_fusion.2), channel_id=1, source_target_pairs={{32,64},{33,65},{34,66},{35,67},{36,68},{37,69},{38,70},{39,71},{4... | collective-permute-start | bytes 294920 | tf_op jit(solution)/shard_map/ppermute | solution.py:575
  169.6 8.6 %collective-permute-start.25 = (bf16[128,384]{1,0:T(8,128)(2,1)S(1)}, bf16[128,384]{1,0:T(8,128)(2,1)S(1)}, u32[]{:S(2)}, u32[]{:S(2)}) collective-permute-start(bf16[128,384]{1,0:T(8,128)(2,1)S(1)} %add.47), channel_id=1, source_target_pairs={{0,16},{32,48},{64,80},{96,112},{1,17},{33,49},{65,81},{97,113},{2... | collective-permute-start | bytes 294920 | tf_op jit(solution)/shard_map/ppermute | solution.py:575
